TPU v7x, 32 devices: a whole 2x2x4 slice. The times are simulated.
32 devices in a mesh: leaf: 8 (over z, x), vec: 4 (over y, core).
Axes of the slice: x: 2, y: 2, z: 4, core: 2. Of those that a mesh axis runs over, the one named last changes fastest.
Arguments:
- panels: float32 [32, 65536], P('vec', 'leaf'), may hold values from -6 to 6
- near_tiles: float32 [512, 4, 128, 128], P('leaf', None, 'vec'), may hold values from -0.25 to 0.25
- near_cols: int32 [512, 4], P('leaf'), may hold values from 0 to 511, as said below
- leaf_order: int32 [512, 128], P('leaf'), may hold values from 0 to 127, each once within a row
- leaf_basis: float32 [512, 64, 128], P('leaf'), may hold values from -0.5 to 0.5
- local_mats: float32 [8, 63, 64, 128], P('leaf'), may hold values from -0.75 to 0.75
- local_flags: int32 [8, 63], P('leaf'), may hold values 0 or 1
- cross_coupling: float32 [6, 64, 64], replicated, may hold values from -0.75 to 0.75
- cross_transfer: float32 [4, 64, 64], replicated, may hold values from -0.75 to 0.75
- cross_flags: int32 [6], replicated, may hold values 0 or 1
Outputs:
- product: float32 [32, 65536], P('vec', 'leaf')
Inputs may be any that keep to these rules, and one draw needn't show every extreme that they name: `near_cols`: every entry of row i names a leaf within 8 leaves of leaf i. `leaf_order`: each row is a permutation of 0 to 127.
All inputs are finite; a program needn't handle non-finite values. No bound on the sum of `local_flags` on one device may be relied on, other than what follows from the above.
Results may differ from a plain program's by a relative error of at most 0.00022.
Values sent between devices are 32-bit elements; how exact they have to be, the bound alone decides.
A program may use at most 64 MiB of HBM per device.

v0:
```python
import math

import jax
import jax.numpy as jnp
from jax import lax
from jax.sharding import PartitionSpec as P

W = 8


precise = lax.Precision.HIGHEST
root_half = 1.0 / math.sqrt(2.0)


def extended_2(cells, sides, width):
    for axis, dim in sides:
        count = lax.axis_size(axis)
        ends = count - 1
        head = lax.slice_in_dim(cells, 0, width, axis=dim)
        tail = lax.slice_in_dim(cells, cells.shape[dim] - width, cells.shape[dim], axis=dim)
        cells = jnp.concatenate(
            [
                lax.ppermute(tail, axis, [(i, (i + 1) % count) for i in range(ends)]),
                cells,
                lax.ppermute(head, axis, [((i + 1) % count, i) for i in range(ends)]),
            ],
            axis=dim,
        )
    return cells


def partner(block, axis, bit):
    count = lax.axis_size(axis)
    route = []
    for low in range(count):
        high = low | 1 << bit
        if high != low and high < count:
            route += [(low, high), (high, low)]
    return lax.ppermute(block, axis, route)


def near_product(tile_rows, sources):
    return jnp.einsum("lnqp,slnp->slq", tile_rows, sources, precision=precise)


def local(
    panels,
    near_tiles,
    near_cols,
    leaf_order,
    leaf_basis,
    local_mats,
    local_flags,
    cross_coupling,
    cross_transfer,
    cross_flags,
):
    rhs_dev = panels.shape[0]
    leaves = leaf_basis.shape[0]
    skel_rank = leaf_basis.shape[1]
    leaf_size = leaf_basis.shape[2]
    halo_cells = W * leaf_size
    leaf_count = lax.axis_size("leaf")
    leaf_index = lax.axis_index("leaf")
    cross_depth = leaf_count.bit_length() - 1
    places = jnp.arange(leaf_size, dtype=jnp.int32)
    order_hot = (leaf_order[:, :, None] == places[None, None, :]).astype(jnp.float32)
    ordered = jnp.einsum(
        "lpm,slm->slp", order_hot, panels.reshape(rhs_dev, leaves, leaf_size), precision=precise
    )
    ordered_flat = ordered.reshape(rhs_dev, leaves * leaf_size)
    local_cols = near_cols - leaf_index * leaves + W
    rim_leaves = jnp.arange(leaves + 2 * W, dtype=jnp.int32)
    select_hot = (local_cols[:, :, None] == rim_leaves[None, None, :]).astype(jnp.float32)
    gathered = lax.all_gather(ordered_flat, "vec", axis=0, tiled=True)
    extended = extended_2(gathered, (("leaf", 1),), halo_cells)
    blocked = extended.reshape(extended.shape[0], leaves + 2 * W, leaf_size)
    partial_rows = near_product(
        near_tiles, jnp.einsum("lne,sep->slnp", select_hot, blocked, precision=precise)
    )
    near_field = lax.all_to_all(partial_rows, "vec", split_axis=0, concat_axis=2, tiled=True)
    local_blocks = local_mats[0]
    local_admit = local_flags[0].astype(jnp.float32)
    leaf_skel = jnp.einsum("lkp,slp->lsk", leaf_basis, ordered, precision=precise)
    skeleton = leaf_skel.reshape(leaves // 2, 2, rhs_dev, skel_rank).sum(axis=1) * root_half
    local_depth = leaves.bit_length() - 1
    coupled = []
    for tree_level in range(1, local_depth):
        node_count = leaves >> tree_level
        first_node = leaves - (leaves >> tree_level - 1)
        blocks = local_blocks[first_node : first_node + node_count]
        sibling = skeleton.reshape(node_count // 2, 2, rhs_dev, skel_rank)[:, ::-1].reshape(
            skeleton.shape
        )
        term = jnp.einsum("jkm,jsm->jsk", blocks[:, :, :skel_rank], sibling, precision=precise)
        coupled.append(local_admit[first_node : first_node + node_count, None, None] * term)
        lifted = jnp.einsum("jsk,jkm->jsm", skeleton, blocks[:, :, skel_rank:], precision=precise)
        skeleton = lifted.reshape(node_count // 2, 2, rhs_dev, skel_rank).sum(axis=1) * root_half
    device_block = local_blocks[leaves - 2]
    device_skel = skeleton[0]
    device_lift = jnp.dot(device_skel, device_block[:, skel_rank:], precision=precise)

    def cross_index(level_bit):
        return leaf_count - (leaf_count >> level_bit - 1) + (leaf_index >> level_bit)

    def transfer_at(level_bit):
        if level_bit == 0:
            return device_block[:, skel_rank:]
        return lax.dynamic_index_in_dim(cross_transfer, cross_index(level_bit), 0, keepdims=False)

    cross_terms = []
    current, carried = (device_skel, device_lift)
    for level_bit in range(cross_depth):
        sibling_skel, sibling_up = partner((current, carried), "leaf", level_bit)
        if level_bit == 0:
            coupling = device_block[:, :skel_rank]
            admitted = local_admit[leaves - 2]
        else:
            node_index = cross_index(level_bit)
            coupling = lax.dynamic_index_in_dim(cross_coupling, node_index, 0, keepdims=False)
            admitted = lax.dynamic_index_in_dim(cross_flags, node_index, 0, keepdims=False).astype(
                jnp.float32
            )
        cross_terms.append(admitted * jnp.dot(sibling_skel, coupling.T, precision=precise))
        if level_bit < cross_depth - 1:
            current = (carried + sibling_up) * root_half
            if level_bit + 1 <= cross_depth - 2:
                carried = jnp.dot(current, transfer_at(level_bit + 1), precision=precise)
    downward = cross_terms[cross_depth - 1]
    for level_bit in range(cross_depth - 2, -1, -1):
        downward = cross_terms[level_bit] + jnp.dot(
            downward, transfer_at(level_bit).T, precision=precise
        )
    downward = downward[None]
    for tree_level in range(local_depth - 1, 0, -1):
        node_count = leaves >> tree_level
        first_node = leaves - (leaves >> tree_level - 1)
        transfer = local_blocks[first_node : first_node + node_count, :, skel_rank:]
        spread = jnp.repeat(downward, 2, axis=0)
        downward = coupled[tree_level - 1] + jnp.einsum(
            "jkm,jsm->jsk", transfer, spread, precision=precise
        )
    far_field = jnp.einsum(
        "lkp,lsk->slp", leaf_basis, jnp.repeat(downward, 2, axis=0), precision=precise
    )
    combined = near_field + far_field
    restored = jnp.einsum("lpm,slp->slm", order_hot, combined, precision=precise)
    return restored.reshape(rhs_dev, leaves * leaf_size)


def solution(mesh):
    return jax.shard_map(
        local,
        mesh=mesh,
        in_specs=(
            P("vec", "leaf"),
            P("leaf", None, "vec", None),
            P("leaf", None),
            P("leaf", None),
            P("leaf", None, None),
            P("leaf", None, None, None),
            P("leaf", None),
            P(),
            P(),
            P(),
        ),
        out_specs=P("vec", "leaf"),
        check_vma=False,
    )
```

profile of v0, /device:TPU:0, one launch (start us, length us, event | category | flops | bytes accessed | tf_op | source)
XLA Modules:
  0.0 107.7 jit_solution(1029454340300619483)
XLA Ops:
  6.5 1.4 %slice_bitcast_fusion = f32[32,64,128]{2,1,0:T(8,128)S(1)} fusion(f32[1,63,64,128]{3,2,1,0:T(8,128)} %param.15), kind=kLoop, calls=%fused_computation.34 | loop fusion | bytes 2097152 | tf_op jit(solution)/shard_map/slice | solution.py:91
  8.0 1.1 %slice_bitcast_fusion.1 = f32[16,64,128]{2,1,0:T(8,128)S(1)} fusion(f32[1,63,64,128]{3,2,1,0:T(8,128)} %param.15), kind=kLoop, calls=%fused_computation.39 | loop fusion | bytes 1048576 | tf_op jit(solution)/shard_map/slice | solution.py:91
  9.1 1.2 %slice_bitcast_fusion.2 = f32[8,64,128]{2,1,0:T(8,128)S(1)} fusion(f32[1,63,64,128]{3,2,1,0:T(8,128)} %param.15), kind=kLoop, calls=%fused_computation.48 | loop fusion | bytes 524288 | tf_op jit(solution)/shard_map/slice | solution.py:91
  10.3 0.9 slice_bitcast_fusion.3
  11.2 0.9 slice_bitcast_fusion.4
  12.1 4.7 %fusion.2 = f32[64,128,8]{1,2,0:T(8,128)S(1)} fusion(s32[64,128]{1,0:T(8,128)S(1)} %copy-done.18, f32[8,8192]{1,0:T(8,128)S(1)} %copy-done.17), kind=kOutput, calls=%fused_computation.4 | convolution fusion | flops 101711872 | bytes 557056 | tf_op jit(solution)/shard_map/lpm,slm->slp/dot_general | solution.py:68
  16.9 3.4 %bitcast_reduce_fusion = f32[32,8,64]{2,1,0:T(8,128)S(1)} fusion(f32[64,64,128]{2,1,0:T(8,128)S(1)} %copy-done, f32[64,128,8]{1,2,0:T(8,128)S(1)} %fusion.2), kind=kOutput, calls=%fused_computation.44 | convolution fusion | flops 50348032 | bytes 2424832 | tf_op jit(solution)/shard_map/lkp,slp->lsk/dot_general | solution.py:84
  20.2 1.2 %bitcast_reduce_fusion.1 = f32[16,8,64]{2,1,0:T(8,128)S(1)} fusion(f32[32,64,128]{2,1,0:T(8,128)S(1)} %slice_bitcast_fusion, f32[32,8,64]{2,1,0:T(8,128)S(1)} %bitcast_reduce_fusion), kind=kOutput, calls=%fused_computation.53 | convolution fusion | flops 12607488 | bytes 1146880 | tf_op jit(solution)/shard_map/jsk,jkm->jsm/dot_general | solution.py:97
  21.4 0.7 bitcast_reduce_fusion.2
  22.1 0.4 bitcast_reduce_fusion.3
  22.5 0.3 bitcast_reduce_fusion.4
  22.8 0.8 fusion.12
  23.7 3.0 %collective-permute-start.2 = (f32[8,64]{1,0:T(8,128)}, f32[8,64]{1,0:T(8,128)}, u32[]{:S(2)}, u32[]{:S(2)}) collective-permute-start(f32[8,64]{1,0:T(8,128)} %fusion.12), channel_id=1, source_target_pairs={{0,4},{4,0},{8,12},{12,8},{16,20},{20,16},{24,28},{28,24},{1,5},{5... | collective-permute-start | bytes 6152 | tf_op jit(solution)/shard_map/ppermute | solution.py:39
  26.6 0.8 slice_bitcast_fusion.5
  27.4 0.6 copy-done.9
  28.0 1.5 %fusion.68 = f32[8,64]{1,0:T(8,128)} fusion(f32[8,64]{1,0:T(8,128)} %fusion.12, f32[64,128]{1,0:T(8,128)S(1)} %slice_bitcast_fusion.5), kind=kOutput, calls=%fused_computation.84 | convolution fusion | flops 393216 | bytes 36864 | tf_op jit(solution)/shard_map/dot_general | solution.py:101
  29.5 0.7 convert_element_type.18
  30.2 0.1 slice_bitcast_fusion.7
  30.4 0.8 reverse_multiply_fusion.2
  31.2 0.8 reverse_multiply_fusion.1
  32.1 1.9 %convolution_multiply_fusion.3 = f32[4,8,64]{2,1,0:T(8,128)} fusion(f32[4,8,64]{2,1,0:T(8,128)S(1)} %bitcast.147, f32[4,64,128]{2,1,0:T(8,128)} %copy-done.4, f32[4]{0:T(128)S(1)} %slice_bitcast_fusion.7), kind=kOutput, calls=%fused_computation.20 | convolution fusion | flops 1574912 | bytes 147472 | tf_op jit(solution)/shard_map/jkm,jsm->jsk/dot_general | solution.py:95
  33.9 0.5 convolution_multiply_fusion.2
  34.5 2.0 %convolution_multiply_fusion.1 = f32[16,8,64]{2,1,0:T(8,128)S(1)} fusion(f32[16,8,64]{2,1,0:T(8,128)S(1)} %bitcast.142, f32[16,64,128]{2,1,0:T(8,128)} %copy-done.1, f32[16]{0:T(128)S(1)} %slice_bitcast_fusion.9), kind=kOutput, calls=%fused_computation.16 | convolution fusion | flops 6299648 | bytes 589888 | tf_op jit(solution)/shard_map/jkm,jsm->jsk/dot_general | solution.py:95
  36.5 1.8 %convolution_multiply_fusion = f32[32,8,64]{2,1,0:T(8,128)S(1)} fusion(f32[32,8,64]{2,1,0:T(8,128)S(1)} %bitcast.139, f32[32,64,128]{2,1,0:T(8,128)S(1)} %slice_bitcast_fusion, f32[32]{0:T(128)S(1)} %slice_bitcast_fusion.10), kind=kOutput, calls=%fused_computation.14 | convolution fusion | flops 12599296 | bytes 1179776 | tf_op jit(solution)/shard_map/jkm,jsm->jsk/dot_general | solution.py:95
  38.3 0.7 add_multiply_fusion.1
  39.0 0.9 fusion.55
  39.9 2.1 %collective-permute-start.5 = (f32[8,64]{1,0:T(8,128)S(1)}, f32[8,64]{1,0:T(8,128)S(1)}, u32[]{:S(2)}, u32[]{:S(2)}) collective-permute-start(f32[8,64]{1,0:T(8,128)S(1)} %fusion.55), channel_id=1, source_target_pairs={{0,8},{8,0},{4,12},{12,4},{16,24},{24,16},{20,28},{28,20},{1,9},{9... | collective-permute-start | bytes 6152 | tf_op jit(solution)/shard_map/ppermute | solution.py:39
  42.0 0.2 convolution_multiply_fusion.4
  42.2 1.4 %collective-permute-done.5 = f32[8,64]{1,0:T(8,128)S(1)} collective-permute-done((f32[8,64]{1,0:T(8,128)S(1)}, f32[8,64]{1,0:T(8,128)S(1)}, u32[]{:S(2)}, u32[]{:S(2)}) %collective-permute-start.5) | collective-permute-done | bytes 2080 | tf_op jit(solution)/shard_map/ppermute | solution.py:39
  43.6 3.0 %collective-permute-start.6 = (f32[8,64]{1,0:T(8,128)S(1)}, f32[8,64]{1,0:T(8,128)S(1)}, u32[]{:S(2)}, u32[]{:S(2)}) collective-permute-start(f32[8,64]{1,0:T(8,128)S(1)} %add_multiply_fusion), channel_id=1, source_target_pairs={{0,16},{16,0},{4,20},{20,4},{8,24},{24,8},{12,28},{28,12},{1,17},{... | collective-permute-start | bytes 6152 | tf_op jit(solution)/shard_map/ppermute | solution.py:39
  46.6 1.2 %slice.157 = f32[1,1]{1,0:T(1,128)} slice(f32[1,63]{1,0:T(1,128)} %copy-done.20), slice={[0:1], [62:63]} | slice | bytes 8 | tf_op jit(solution)/shard_map/slice | solution.py:117
  47.9 0.6 fusion.95
  49.8 1.6 %collective-permute-start.4 = (f32[8,64]{1,0:T(8,128)S(1)}, f32[8,64]{1,0:T(8,128)S(1)}, u32[]{:S(2)}, u32[]{:S(2)}) collective-permute-start(f32[8,64]{1,0:T(8,128)S(1)} %add_multiply_fusion.1), channel_id=1, source_target_pairs={{0,8},{8,0},{4,12},{12,4},{16,24},{24,16},{20,28},{28,20},{1,9},{9... | collective-permute-start | bytes 6152 | tf_op jit(solution)/shard_map/ppermute | solution.py:39
  51.4 0.9 convolution_multiply_fusion.5
  52.3 0.9 fusion.53
  53.2 0.2 collective-permute-done.4
  53.4 0.9 fusion.10
  54.3 0.2 fusion.66
  54.6 1.4 %fusion.11 = f32[8,64]{1,0:T(8,128)S(1)} fusion(f32[8,64]{1,0:T(8,128)S(1)} %fusion.66, f32[8,64]{1,0:T(8,128)} %collective-permute-done.2, f32[64,128]{1,0:T(8,128)S(1)} %copy-done.10, f32[]{:T(128)} %bitcast.35), kind=kOutput, calls=%fused_computation.27 | convolution fusion | flops 394240 | bytes 38916 | tf_op jit(solution)/shard_map/dot_general | solution.py:124
  56.0 1.1 %convolution_add_fusion.4 = f32[2,8,64]{2,1,0:T(8,128)S(1)} fusion(f32[2,8,64]{2,1,0:T(8,128)S(1)} %convolution_multiply_fusion.4, f32[63,64,128]{2,1,0:T(8,128)} %bitcast.126, f32[8,64]{1,0:T(8,128)S(1)} %fusion.11), kind=kOutput, calls=%fused_computation.21 | convolution fusion | flops 787456 | bytes 75776 | tf_op jit(solution)/shard_map/jkm,jsm->jsk/dot_general | solution.py:140
  57.1 1.3 %convolution_add_fusion.3 = f32[4,8,64]{2,1,0:T(8,128)S(1)} fusion(f32[4,8,64]{2,1,0:T(8,128)S(1)} %copy-done.14, f32[4,8,64]{2,1,0:T(8,128)S(1)} %bitcast.148, f32[63,64,128]{2,1,0:T(8,128)} %bitcast.127), kind=kOutput, calls=%fused_computation.19 | convolution fusion | flops 1574912 | bytes 155648 | tf_op jit(solution)/shard_map/jkm,jsm->jsk/dot_general | solution.py:140
  58.5 1.5 %convolution_add_fusion.2 = f32[8,8,64]{2,1,0:T(8,128)S(1)} fusion(f32[8,8,64]{2,1,0:T(8,128)S(1)} %convolution_multiply_fusion.2, f32[8,8,64]{2,1,0:T(8,128)S(1)} %bitcast.146, f32[63,64,128]{2,1,0:T(8,128)} %bitcast.128), kind=kOutput, calls=%fused_computation.17 | convolution fusion | flops 3149824 | bytes 311296 | tf_op jit(solution)/shard_map/jkm,jsm->jsk/dot_general | solution.py:140
  60.0 1.1 fusion.94
  61.1 3.4 %collective-permute-start = (f32[32,1024]{1,0:T(8,128)S(1)}, f32[32,1024]{1,0:T(8,128)S(1)}, u32[]{:S(2)}, u32[]{:S(2)}) collective-permute-start(f32[32,1024]{1,0:T(8,128)S(1)} %get-tuple-element.5), channel_id=1, source_target_pairs={{0,4},{4,8},{8,12},{12,16},{16,20},{20,24},{24,28},{1,5},{5,9},{9,... | collective-permute-start | bytes 393224 | tf_op jit(solution)/shard_map/ppermute | solution.py:23
  64.5 1.5 %collective-permute-start.1 = (f32[32,1024]{1,0:T(8,128)S(1)}, f32[32,1024]{1,0:T(8,128)S(1)}, u32[]{:S(2)}, u32[]{:S(2)}) collective-permute-start(f32[32,1024]{1,0:T(8,128)S(1)} %get-tuple-element.6), channel_id=1, source_target_pairs={{4,0},{8,4},{12,8},{16,12},{20,16},{24,20},{28,24},{5,1},{9,5},{13... | collective-permute-start | bytes 393224 | tf_op jit(solution)/shard_map/ppermute | solution.py:25
  66.0 2.0 %convolution_add_fusion.1 = f32[16,8,64]{2,1,0:T(8,128)S(1)} fusion(f32[16,8,64]{2,1,0:T(8,128)S(1)} %convolution_multiply_fusion.1, f32[16,8,64]{2,1,0:T(8,128)S(1)} %bitcast.143, f32[63,64,128]{2,1,0:T(8,128)} %bitcast.129), kind=kOutput, calls=%fused_computation.15 | convolution fusion | flops 6299648 | bytes 622592 | tf_op jit(solution)/shard_map/jkm,jsm->jsk/dot_general | solution.py:140
  68.1 0.3 collective-permute-done
  68.4 3.0 %collective-permute-done.1 = f32[32,1024]{1,0:T(8,128)S(1)} collective-permute-done((f32[32,1024]{1,0:T(8,128)S(1)}, f32[32,1024]{1,0:T(8,128)S(1)}, u32[]{:S(2)}, u32[]{:S(2)}) %collective-permute-start.1) | collective-permute-done | bytes 131104 | tf_op jit(solution)/shard_map/ppermute | solution.py:25
  71.4 0.1 maximum_bitcast_fusion
  71.5 0.2 copy.22
  71.7 1.9 %convolution_bitcast_fusion.1 = f32[32,64,4,128]{3,1,2,0:T(8,128)S(1)} fusion(f32[32,80,128,1]{2,1,0,3:T(8,128)S(1)} %bitcast.131, s32[64,4]{0,1:T(4,128)S(1)} %subtract_add_fusion), kind=kOutput, calls=%fused_computation.5 | convolution fusion | flops 1006653440 | bytes 5506048 | tf_op jit(solution)/shard_map/lne,sep->slnp/dot_general | solution.py:79
  73.6 0.3 copy-done.2
  73.9 6.2 %fusion.5 = f32[32,64,32]{2,0,1:T(8,128)S(1)} fusion(f32[64,4,32,128]{3,2,1,0:T(8,128)S(1)} %copy-done.2, f32[32,64,4,128]{3,1,2,0:T(8,128)S(1)} %convolution_bitcast_fusion.1), kind=kOutput, calls=%fused_computation.8 | convolution fusion | flops 402653184 | bytes 8650752 | tf_op jit(solution)/shard_map/lnqp,slnp->slq/dot_general | solution.py:43
  80.1 1.4 %copy.17 = f32[32,64,32]{1,2,0:T(8,128)} copy(f32[32,64,32]{2,0,1:T(8,128)S(1)} %fusion.5) | data formatting | bytes 524288 | tf_op jit(solution)/shard_map/lnqp,slnp->slq/transpose | solution.py:43
  81.5 2.1 %reshape.130 = f32[4,1,16384]{2,1,0:T(1,128)} reshape(f32[32,32,64]{2,1,0:T(8,128)} %bitcast.132) | data formatting | bytes 524288
  83.6 3.6 %all-to-all-start = ((f32[4,1,16384]{2,1,0:T(1,128)}), f32[4,1,16384]{2,1,0:T(1,128)S(1)}, u32[]{:S(2)}, u32[]{:S(2)}) async-start(f32[4,1,16384]{2,1,0:T(1,128)} %reshape.130), calls=%async_computation | async-start | bytes 524288 | tf_op jit(solution)/shard_map/all_to_all | solution.py:81
  87.2 3.0 %convolution_add_fusion = f32[32,8,64]{2,1,0:T(8,128)S(1)} fusion(f32[32,8,64]{2,1,0:T(8,128)S(1)} %convolution_multiply_fusion, f32[32,8,64]{2,1,0:T(8,128)S(1)} %bitcast.140, f32[63,64,128]{2,1,0:T(8,128)} %bitcast.130), kind=kOutput, calls=%fused_computation.13 | convolution fusion | flops 12599296 | bytes 1245184 | tf_op jit(solution)/shard_map/jkm,jsm->jsk/dot_general | solution.py:140
  90.3 2.7 %all-to-all-done = f32[4,1,16384]{2,1,0:T(1,128)S(1)} async-done(((f32[4,1,16384]{2,1,0:T(1,128)}), f32[4,1,16384]{2,1,0:T(1,128)S(1)}, u32[]{:S(2)}, u32[]{:S(2)}) %all-to-all-start) | async-done | bytes 262176 | tf_op jit(solution)/shard_map/all_to_all | solution.py:81
  93.0 0.5 broadcast.17
  93.5 1.4 %reduce.2 = f32[4,16384]{1,0:T(4,128)S(1)} reduce(f32[4,1,16384]{2,1,0:T(1,128)S(1)} %all-to-all-done, f32[]{:T(128)} %broadcast.17), dimensions={1}, to_apply=%all_to_all.13.reduce_sub_computation | reduce | bytes 524292 | tf_op jit(solution)/shard_map/all_to_all | solution.py:81
  94.8 0.3 reshape.131
  95.2 0.2 copy.19
  95.4 1.9 %fusion.9 = f32[8,64,128]{2,0,1:T(8,128)S(1)} fusion(f32[8,64,128]{2,0,1:T(8,128)S(1)} %copy.19, f32[64,8,64]{2,1,0:T(8,128)S(1)} %bitcast.137, f32[64,64,128]{2,1,0:T(8,128)S(1)} %copy-done), kind=kOutput, calls=%fused_computation.12 | convolution fusion | flops 50397184 | bytes 2752512 | tf_op jit(solution)/shard_map/lkp,lsk->slp/dot_general | solution.py:143
  97.3 3.6 %convolution_bitcast_fusion = f32[8,8192]{1,0:T(8,128)} fusion(f32[8,64,128]{2,0,1:T(8,128)S(1)} %fusion.9, s32[64,128]{1,0:T(8,128)S(1)} %copy-done.19), kind=kOutput, calls=%fused_computation | convolution fusion | flops 101711872 | bytes 557056 | tf_op jit(solution)/shard_map/lpm,slp->slm/dot_general | solution.py:147
  (62 shorter events, 0.5 us)
Async XLA Ops:
  6.5 10.3 %copy-start = (f32[64,64,128]{2,1,0:T(8,128)S(1)}, f32[64,64,128]{2,1,0:T(8,128)}, u32[]{:S(2)}) copy-start(f32[64,64,128]{2,1,0:T(8,128)} %param.14) | copy-start | bytes 6291460
  6.5 5.5 %copy-start.18 = (s32[64,128]{1,0:T(8,128)S(1)}, s32[64,128]{1,0:T(8,128)}, u32[]{:S(2)}) copy-start(s32[64,128]{1,0:T(8,128)} %param.13) | copy-start | bytes 98308
  6.5 53.5 %all-gather.2.cloned.1.call-start = ((), (), s32[]{:S(2)}) async-start(), calls=%async_computation.1 | async-start | bytes 1310720 | tf_op jit(solution)/shard_map/all_gather | solution.py:75
  6.5 5.5 %copy-start.17 = (f32[8,8192]{1,0:T(8,128)S(1)}, f32[8,8192]{1,0:T(8,128)}, u32[]{:S(2)}) copy-start(f32[8,8192]{1,0:T(8,128)} %param.10) | copy-start | bytes 786436
  9.1 12.3 %copy-start.1 = (f32[16,64,128]{2,1,0:T(8,128)}, f32[16,64,128]{2,1,0:T(8,128)S(1)}, u32[]{:S(2)}) copy-start(f32[16,64,128]{2,1,0:T(8,128)S(1)} %slice_bitcast_fusion.1) | copy-start | bytes 1572868
  11.2 11.3 %copy-start.4 = (f32[4,64,128]{2,1,0:T(8,128)}, f32[4,64,128]{2,1,0:T(8,128)S(1)}, u32[]{:S(2)}) copy-start(f32[4,64,128]{2,1,0:T(8,128)S(1)} %slice_bitcast_fusion.3) | copy-start | bytes 393220
  12.1 10.7 %copy-start.7 = (f32[2,64,128]{2,1,0:T(8,128)}, f32[2,64,128]{2,1,0:T(8,128)S(1)}, u32[]{:S(2)}) copy-start(f32[2,64,128]{2,1,0:T(8,128)S(1)} %slice_bitcast_fusion.4) | copy-start | bytes 196612
  16.9 5.2 %copy-start.5 = (f32[64,128,8]{1,2,0:T(8,128)}, f32[64,128,8]{1,2,0:T(8,128)S(1)}, u32[]{:S(2)}) copy-start(f32[64,128,8]{1,2,0:T(8,128)S(1)} %fusion.2) | copy-start | bytes 786436
  21.4 1.4 %copy-start.6 = (f32[16,8,64]{2,1,0:T(8,128)}, f32[16,8,64]{2,1,0:T(8,128)S(1)}, u32[]{:S(2)}) copy-start(f32[16,8,64]{2,1,0:T(8,128)S(1)} %bitcast_reduce_fusion.1) | copy-start | bytes 98308
  22.1 1.6 %copy-start.11 = (f32[8,8,64]{2,1,0:T(8,128)}, f32[8,8,64]{2,1,0:T(8,128)S(1)}, u32[]{:S(2)}) copy-start(f32[8,8,64]{2,1,0:T(8,128)S(1)} %bitcast_reduce_fusion.2) | copy-start | bytes 49156
  22.8 6.7 %copy-start.12 = (f32[2,8,64]{2,1,0:T(8,128)}, f32[2,8,64]{2,1,0:T(8,128)S(1)}, u32[]{:S(2)}) copy-start(f32[2,8,64]{2,1,0:T(8,128)S(1)} %bitcast_reduce_fusion.4) | copy-start | bytes 12292
  23.7 30.9 %collective-permute-start.2 = (f32[8,64]{1,0:T(8,128)}, f32[8,64]{1,0:T(8,128)}, u32[]{:S(2)}, u32[]{:S(2)}) collective-permute-start(f32[8,64]{1,0:T(8,128)} %fusion.12), channel_id=1, source_target_pairs={{0,4},{4,0},{8,12},{12,8},{16,20},{20,16},{24,28},{28,24},{1,5},{5... | collective-permute-start | bytes 6152 | tf_op jit(solution)/shard_map/ppermute | solution.py:39
  27.4 0.6 copy-start.9
  29.5 8.8 %collective-permute-start.3 = (f32[8,64]{1,0:T(8,128)}, f32[8,64]{1,0:T(8,128)}, u32[]{:S(2)}, u32[]{:S(2)}) collective-permute-start(f32[8,64]{1,0:T(8,128)} %fusion.68), channel_id=1, source_target_pairs={{0,4},{4,0},{8,12},{12,8},{16,20},{20,16},{24,28},{28,24},{1,5},{5... | collective-permute-start | bytes 6152 | tf_op jit(solution)/shard_map/ppermute | solution.py:39
  30.2 8.1 %copy-start.20 = (f32[1,63]{1,0:T(1,128)}, f32[1,63]{1,0:T(1,128)S(1)}, u32[]{:S(2)}) copy-start(f32[1,63]{1,0:T(1,128)S(1)} %convert_element_type.18) | copy-start | bytes 760
  30.4 7.9 %copy-start.13 = (f32[2,8,64]{2,1,0:T(8,128)S(1)}, f32[2,8,64]{2,1,0:T(8,128)}, u32[]{:S(2)}) copy-start(f32[2,8,64]{2,1,0:T(8,128)} %copy-done.12) | copy-start | bytes 12292
  30.4 16.2 %copy-start.16 = (s32[64,4]{0,1:T(4,128)S(1)}, s32[64,4]{0,1:T(4,128)}, u32[]{:S(2)}) copy-start(s32[64,4]{0,1:T(4,128)} %param.12) | copy-start | bytes 3076
  30.4 17.5 %copy-start.15 = (s32[6]{0:T(128)S(1)}, s32[6]{0:T(128)}, u32[]{:S(2)}) copy-start(s32[6]{0:T(128)} %param.19) | copy-start | bytes 76
  32.1 9.9 %copy-start.8 = (f32[2,64,128]{2,1,0:T(8,128)S(1)}, f32[2,64,128]{2,1,0:T(8,128)}, u32[]{:S(2)}) copy-start(f32[2,64,128]{2,1,0:T(8,128)} %copy-done.7) | copy-start | bytes 196612
  32.1 22.2 %copy-start.10 = (f32[64,128]{1,0:T(8,128)S(1)}, f32[64,128]{1,0:T(8,128)}, u32[]{:S(2)}) copy-start(f32[64,128]{1,0:T(8,128)} %copy-done.9) | copy-start | bytes 98308
  34.5 22.7 %copy-start.14 = (f32[4,8,64]{2,1,0:T(8,128)S(1)}, f32[4,8,64]{2,1,0:T(8,128)}, u32[]{:S(2)}) copy-start(f32[4,8,64]{2,1,0:T(8,128)} %convolution_multiply_fusion.3) | copy-start | bytes 24580
  39.9 3.7 %collective-permute-start.5 = (f32[8,64]{1,0:T(8,128)S(1)}, f32[8,64]{1,0:T(8,128)S(1)}, u32[]{:S(2)}, u32[]{:S(2)}) collective-permute-start(f32[8,64]{1,0:T(8,128)S(1)} %fusion.55), channel_id=1, source_target_pairs={{0,8},{8,0},{4,12},{12,4},{16,24},{24,16},{20,28},{28,20},{1,9},{9... | collective-permute-start | bytes 6152 | tf_op jit(solution)/shard_map/ppermute | solution.py:39
  43.6 7.8 %collective-permute-start.6 = (f32[8,64]{1,0:T(8,128)S(1)}, f32[8,64]{1,0:T(8,128)S(1)}, u32[]{:S(2)}, u32[]{:S(2)}) collective-permute-start(f32[8,64]{1,0:T(8,128)S(1)} %add_multiply_fusion), channel_id=1, source_target_pairs={{0,16},{16,0},{4,20},{20,4},{8,24},{24,8},{12,28},{28,12},{1,17},{... | collective-permute-start | bytes 6152 | tf_op jit(solution)/shard_map/ppermute | solution.py:39
  49.8 3.7 %collective-permute-start.4 = (f32[8,64]{1,0:T(8,128)S(1)}, f32[8,64]{1,0:T(8,128)S(1)}, u32[]{:S(2)}, u32[]{:S(2)}) collective-permute-start(f32[8,64]{1,0:T(8,128)S(1)} %add_multiply_fusion.1), channel_id=1, source_target_pairs={{0,8},{8,0},{4,12},{12,4},{16,24},{24,16},{20,28},{28,20},{1,9},{9... | collective-permute-start | bytes 6152 | tf_op jit(solution)/shard_map/ppermute | solution.py:39
  60.0 11.4 %copy-start.3 = (f32[32,8192]{1,0:T(8,128)S(1)}, f32[32,8192]{1,0:T(8,128)}, u32[]{:S(2)}) copy-start(f32[32,8192]{1,0:T(8,128)} %all-gather.2.cloned.1.call-done) | copy-start | bytes 3145732
  61.1 7.3 %collective-permute-start = (f32[32,1024]{1,0:T(8,128)S(1)}, f32[32,1024]{1,0:T(8,128)S(1)}, u32[]{:S(2)}, u32[]{:S(2)}) collective-permute-start(f32[32,1024]{1,0:T(8,128)S(1)} %get-tuple-element.5), channel_id=1, source_target_pairs={{0,4},{4,8},{8,12},{12,16},{16,20},{20,24},{24,28},{1,5},{5,9},{9,... | collective-permute-start | bytes 393224 | tf_op jit(solution)/shard_map/ppermute | solution.py:23
  64.5 6.9 %collective-permute-start.1 = (f32[32,1024]{1,0:T(8,128)S(1)}, f32[32,1024]{1,0:T(8,128)S(1)}, u32[]{:S(2)}, u32[]{:S(2)}) collective-permute-start(f32[32,1024]{1,0:T(8,128)S(1)} %get-tuple-element.6), channel_id=1, source_target_pairs={{4,0},{8,4},{12,8},{16,12},{20,16},{24,20},{28,24},{5,1},{9,5},{13... | collective-permute-start | bytes 393224 | tf_op jit(solution)/shard_map/ppermute | solution.py:25
  71.7 2.2 %copy-start.2 = (f32[64,4,32,128]{3,2,1,0:T(8,128)S(1)}, f32[64,4,32,128]{3,2,1,0:T(8,128)}, u32[]{:S(2)}) copy-start(f32[64,4,32,128]{3,2,1,0:T(8,128)} %param.11) | copy-start | bytes 12582916
  83.6 9.4 %all-to-all-start = ((f32[4,1,16384]{2,1,0:T(1,128)}), f32[4,1,16384]{2,1,0:T(1,128)S(1)}, u32[]{:S(2)}, u32[]{:S(2)}) async-start(f32[4,1,16384]{2,1,0:T(1,128)} %reshape.130), calls=%async_computation | async-start | bytes 524288 | tf_op jit(solution)/shard_map/all_to_all | solution.py:81
  95.2 2.1 %copy-start.19 = (s32[64,128]{1,0:T(8,128)S(1)}, s32[64,128]{1,0:T(8,128)}, u32[]{:S(2)}) copy-start(s32[64,128]{1,0:T(8,128)} %param.13) | copy-start | bytes 98308
Sparse Core Ops, SparseCore 0:
  29.6 18.5 all-gather.1
where the time goes:
time: 109 us; the launch traced here: 108 us
  matrix products  47.1 us (43%)
  starting transfers between devices  18.3 us (17%)
  local copies, waits for them, and re-layouts  15.3 us (14%)
  between operations  15 us (14%)
  waiting for transfers between devices  7.65 us (7%)
  other arithmetic  4.46 us (4%)
    ppermute x5, starting transfers between devices, partner(): return lax.ppermute(block, axis, route)  9.76 us
    dot_general x5, matrix products, local(): jnp.einsum('jkm,jsm->jsk', transfer, spread, precision=precise)  9.07 us
    dot_general x5, matrix products, local(): jnp.einsum('jkm,jsm->jsk', blocks[:, :, :skel_rank], sibling, precision=p...  6.3 us
    dot_general x1, matrix products, near_product(): return jnp.einsum('lnqp,slnp->slq', tile_rows, sources, precision=precise)  6.21 us
    slice x5, local copies, waits for them, and re-layouts, local(): blocks = local_blocks[first_node:first_node + node_count]  5.5 us
    dot_general x1, matrix products, local(): jnp.einsum('lpm,slm->slp', order_hot, panels.reshape(rhs_dev, leaves, lea...  4.75 us
    all_to_all x1, starting transfers between devices, local(): lax.all_to_all(partial_rows, 'vec', split_axis=0, concat_axis=2, tiled=True)  3.63 us
    unnamed x45, local copies, waits for them, and re-layouts  3.58 us
  transfers between devices with their start and end apart: 9, of which 5 were waited for; matrix products, arithmetic and copies ran while one was open for 26% of the time, Pallas kernels for 0%

commit v1 on v0

v1 whole, which is shorter than its diff:
```python
import functools
import math

import jax
import jax.numpy as jnp
from jax import lax
from jax.experimental import pallas as pl
from jax.experimental.pallas import tpu as pltpu
from jax.sharding import PartitionSpec as P

W = 8
f32 = jnp.float32
bf16 = jnp.bfloat16
root_half = 1.0 / math.sqrt(2.0)
MESH = pl.DeviceIdType.MESH
NN = (((1,), (0,)), ((), ()))
NT = (((1,), (1,)), ((), ()))


def halves(x):
    high = x.astype(bf16).astype(f32)
    return high, x - high


def stacked(x):
    return jnp.concatenate(halves(x), axis=0).astype(bf16)


def dot_split(x, w, dims):
    rows = x.shape[0]
    lhs = stacked(x)
    high = w.astype(bf16)
    low = (w - high.astype(f32)).astype(bf16)
    r = lax.dot_general(lhs, high, dims, preferred_element_type=f32) + lax.dot_general(
        lhs, low, dims, preferred_element_type=f32
    )
    return r[:rows] + r[rows:]


def hot_of(order_row):
    size = order_row.shape[1]
    rows = lax.broadcasted_iota(jnp.int32, (size, size), 0)
    return jnp.where(rows == order_row, 1.0, 0.0).astype(bf16)


def order_kernel(panels_ref, order_ref, out_ref):
    leaves, size = order_ref.shape
    span = 8

    def body(i, carry):
        for u in range(span):
            leaf = i * span + u
            hot = hot_of(order_ref[pl.ds(leaf, 1), :])
            x = stacked(panels_ref[:, pl.ds(pl.multiple_of(leaf * size, size), size)])
            r = lax.dot_general(x, hot, NN, preferred_element_type=f32)
            rows = panels_ref.shape[0]
            out_ref[leaf] = r[:rows] + r[rows:]
        return carry

    lax.fori_loop(0, leaves // span, body, 0)


def restore_kernel(far_ref, near_ref, order_ref, out_ref):
    leaves, size = order_ref.shape
    n_vec = near_ref.shape[0]
    piece = size // n_vec
    rows = out_ref.shape[0]
    block = lax.broadcasted_iota(jnp.int32, (rows, size), 1) // piece

    def body(g, carry):
        parts = [near_ref[v, g] for v in range(n_vec)]
        for u in range(n_vec):
            leaf = g * n_vec + u
            near = parts[0] if u == 0 else pltpu.roll(parts[0], (size - u * piece), 1)
            for v in range(1, n_vec):
                shift = ((v - u) * piece) % size
                moved = parts[v] if shift == 0 else pltpu.roll(parts[v], shift, 1)
                near = jnp.where(block == v, moved, near)
            combined = near + far_ref[leaf]
            hot = hot_of(order_ref[pl.ds(leaf, 1), :])
            r = lax.dot_general(stacked(combined), hot, NT, preferred_element_type=f32)
            out_ref[:, pl.ds(pl.multiple_of(leaf * size, size), size)] = r[:rows] + r[rows:]
        return carry

    lax.fori_loop(0, leaves // n_vec, body, 0)


def main_kernel(
    n_leaf,
    n_vec,
    own_ref,
    cols_ref,
    flags_ref,
    cross_flags_ref,
    cross_c_ref,
    cross_e_ref,
    tiles_hbm,
    basis_hbm,
    mats_hbm,
    far_ref,
    near_ref,
    tiles,
    basis,
    mats,
    ext,
    xs,
    hp,
    zp,
    pay,
    hx,
    nout,
    load_sem,
    gs_send,
    gs_recv,
    halo_send,
    halo_recv,
    pay_send,
    pay_recv,
    near_send,
    near_recv,
):
    leaves = own_ref.shape[0]
    rank = 64
    li = lax.axis_index("leaf")
    vi = lax.axis_index("vec")
    load_b = pltpu.make_async_copy(basis_hbm, basis, load_sem.at[0])
    load_m = pltpu.make_async_copy(mats_hbm, mats, load_sem.at[1])
    load_t = pltpu.make_async_copy(tiles_hbm, tiles, load_sem.at[2])
    load_o = pltpu.make_async_copy(own_ref, ext.at[vi, pl.ds(W, leaves)], load_sem.at[3])
    load_b.start()
    load_m.start()
    load_t.start()
    load_o.start()

    right = lax.rem(li + 1, n_leaf)
    left = lax.rem(li + n_leaf - 1, n_leaf)
    barrier = pltpu.get_barrier_semaphore()
    greeted = 0
    for d in range(1, n_vec):
        pl.semaphore_signal(
            barrier, inc=1, device_id=(li, lax.rem(vi + d, n_vec)), device_id_type=MESH
        )
        greeted += 1
    for side in (left, right):
        for u in range(n_vec):
            pl.semaphore_signal(
                barrier, inc=1, device_id=(side, lax.rem(vi + u, n_vec)), device_id_type=MESH
            )
            greeted += 1
    for d in range(2, n_leaf - 1):
        pl.semaphore_signal(
            barrier, inc=1, device_id=(lax.rem(li + d, n_leaf), vi), device_id_type=MESH
        )
        greeted += 1
    pl.semaphore_wait(barrier, greeted)

    def gather_copy(d):
        return pltpu.make_async_remote_copy(
            src_ref=own_ref,
            dst_ref=ext.at[vi, pl.ds(W, leaves)],
            send_sem=gs_send.at[d],
            recv_sem=gs_recv.at[n_vec - d],
            device_id=(li, lax.rem(vi + d, n_vec)),
            device_id_type=MESH,
        )

    def halo_copy(side, d):
        start = leaves - W if side == 0 else 0
        to = 0 if side == 0 else leaves + W
        return pltpu.make_async_remote_copy(
            src_ref=own_ref.at[pl.ds(start, W)],
            dst_ref=ext.at[vi, pl.ds(to, W)],
            send_sem=halo_send.at[side, d],
            recv_sem=halo_recv.at[side, (n_vec - d) % n_vec],
            device_id=(right if side == 0 else left, lax.rem(vi + d, n_vec)),
            device_id_type=MESH,
        )

    gathers = [gather_copy(d) for d in range(1, n_vec)]
    halos = [halo_copy(side, d) for side in range(2) for d in range(n_vec)]
    for c in halos + gathers:
        c.start()

    lane = lax.broadcasted_iota(jnp.int32, (8, 2 * rank), 1)
    low = lane < rank

    def swap(x):
        return pltpu.roll(x, rank, 1)

    load_b.wait()

    def skel_body(i, carry):
        for w in range(2):
            t = i * 2 + w
            sums = []
            for u in range(2):
                pair = t * 2 + u
                x = own_ref[pl.ds(pair * 2, 2)].reshape(16, 128)
                wt = basis[pl.ds(pl.multiple_of(pair * 128, 128), 128), :]
                r = dot_split(x, wt, NT)
                sums.append((r[:8], r[8:]))
            even = sums[0][0] + swap(sums[0][1])
            odd = swap(sums[1][0]) + sums[1][1]
            hp[t] = jnp.where(low, even, odd) * root_half
        return carry

    lax.fori_loop(0, leaves // 8, skel_body, 0)
    load_m.wait()

    def mat_pair(q):
        return mats[pl.ds(pl.multiple_of(q * 128, 128), 128), :]

    def up(off, nxt, t):
        r0 = dot_split(hp[off + 2 * t], mat_pair(off + 2 * t), NN)
        r1 = dot_split(hp[off + 2 * t + 1], mat_pair(off + 2 * t + 1), NN)
        hp[nxt + t] = jnp.where(low, swap(r0), r1) * root_half

    pairs = leaves // 4
    offs = []
    off = 0
    while pairs >= 1:
        offs.append((off, pairs))
        off += pairs
        pairs //= 2
    for (a, count), (b, half) in zip(offs[:-1], offs[1:]):
        if half > 4:
            def up_body(i, carry, a=a, b=b):
                for w in range(4):
                    up(a, b, i * 4 + w)
                return carry

            lax.fori_loop(0, half // 4, up_body, 0)
        else:
            for t in range(half):
                up(a, b, t)
    last = offs[-1][0]
    r = dot_split(hp[last], mat_pair(last), NN)
    skel = swap(r) * root_half
    top = mats[pl.ds((last + 1) * 128, rank), :]
    lift = dot_split(skel[:, :rank], top, NN)
    pay[li] = jnp.where(low, skel, lift)

    def pay_copy(d):
        return pltpu.make_async_remote_copy(
            src_ref=pay.at[li],
            dst_ref=pay.at[li],
            send_sem=pay_send.at[d],
            recv_sem=pay_recv.at[n_leaf - d],
            device_id=(lax.rem(li + d, n_leaf), vi),
            device_id_type=MESH,
        )

    pays = [pay_copy(d) for d in range(1, n_leaf)]
    for c in pays:
        c.start()

    load_o.wait()
    load_t.wait()
    for c in halos + gathers:
        c.wait_recv()
    for c in halos + gathers:
        c.wait_send()

    def split_body(i, carry):
        for w in range(4):
            e = i * 4 + w
            xs[e] = stacked(ext[:, e].reshape(n_vec * 8, 128))
        return carry

    lax.fori_loop(0, (leaves + 2 * W) // 4, split_body, 0)
    base = li * leaves - W
    slots = tiles.shape[1]
    piece = tiles.shape[2]

    def place(leaf, n):
        return jnp.clip(cols_ref[leaf, n] - base, 0, leaves + 2 * W - 1)

    def near_body(g, carry):
        outs = []
        for w in range(n_vec):
            leaf = g * n_vec + w
            x = jnp.concatenate([xs[place(leaf, n)] for n in range(slots)], axis=1)
            t = jnp.concatenate([stacked(tiles[leaf, n]) for n in range(slots)], axis=1)
            r = lax.dot_general(x, t, NT, preferred_element_type=f32)
            half = r.shape[0] // 2
            r = r[:half] + r[half:]
            outs.append(r[:, :piece] + r[:, piece:])
        nout[:, g] = jnp.concatenate(outs, axis=1).reshape(n_vec, 8, n_vec * piece)
        return carry

    lax.fori_loop(0, leaves // n_vec, near_body, 0)

    def near_copy(d):
        u = lax.rem(vi + d, n_vec)
        return pltpu.make_async_remote_copy(
            src_ref=nout.at[u],
            dst_ref=near_ref.at[vi],
            send_sem=near_send.at[d],
            recv_sem=near_recv.at[n_vec - d],
            device_id=(li, u),
            device_id_type=MESH,
        )

    nears = [near_copy(d) for d in range(1, n_vec)]
    for c in nears:
        c.start()
    keep = pltpu.make_async_copy(nout.at[vi], near_ref.at[vi], near_send.at[0])
    keep.start()

    for c in pays:
        c.wait_recv()
    for c in pays:
        c.wait_send()

    depth = n_leaf.bit_length() - 1

    def cross_at(c):
        return n_leaf - (n_leaf >> (c - 1))

    lifts = [pay[j] for j in range(n_leaf)]
    at = 0
    starts = {}
    for c in range(1, depth):
        nodes = [
            (lifts[2 * j] + lifts[2 * j + 1]) * root_half for j in range(len(lifts) // 2)
        ]
        nodes = [swap(x) if c == 1 else x for x in nodes]
        starts[c] = at
        for j, x in enumerate(nodes):
            hx[at + j] = x
        at += len(nodes)
        if c < depth - 1:
            lifts = []
            for j, x in enumerate(nodes):
                y = dot_split(x[:, :rank], cross_e_ref[cross_at(c) + j], NN)
                lifts.append(jnp.concatenate([y, y], axis=1))
    z = None
    for c in range(depth - 1, 0, -1):
        node = li >> c
        sibling = node + 1 - 2 * lax.rem(node, 2)
        spot = cross_at(c) + node
        a = cross_flags_ref[spot].astype(f32)
        g = dot_split(a * hx[starts[c] + sibling][:, :rank], cross_c_ref[spot], NT)
        z = g if z is None else g + dot_split(z, cross_e_ref[spot], NT)
    sibling = li + 1 - 2 * lax.rem(li, 2)
    a = flags_ref[0, 2 * (last + 1)].astype(f32)
    x = jnp.where(low, a * pay[sibling], jnp.concatenate([z, z], axis=1))
    z = dot_split(x, top, NT)
    z = jnp.concatenate([z, z], axis=1)

    def down(q, parent):
        h = hp[q]
        a0 = flags_ref[0, 2 * q].astype(f32)
        a1 = flags_ref[0, 2 * q + 1].astype(f32)
        x0 = jnp.where(low, a0 * swap(h), parent)
        x1 = jnp.where(low, a1 * h, parent)
        r = dot_split(jnp.concatenate([x0, x1], axis=0), mat_pair(q), NT)
        zp[q] = jnp.where(low, r[:8], r[8:])

    down(last, z)
    for (a, count), (b, half) in list(zip(offs[:-1], offs[1:]))[::-1]:
        def down_one(t, a=a, b=b):
            p = zp[b + t]
            down(a + 2 * t, swap(p))
            down(a + 2 * t + 1, p)

        if half > 4:
            def down_body(i, carry, down_one=down_one):
                for w in range(4):
                    down_one(i * 4 + w)
                return carry

            lax.fori_loop(0, half // 4, down_body, 0)
        else:
            for t in range(half):
                down_one(t)

    def far_body(i, carry):
        for w in range(2):
            t = i * 2 + w
            p = zp[t]
            s = swap(p)
            zero = jnp.zeros_like(p)
            for u in range(2):
                pair = 2 * t + u
                first, second = (p, s) if u == 0 else (s, p)
                x = jnp.concatenate(
                    [jnp.where(low, first, zero), jnp.where(low, zero, second)], axis=0
                )
                wt = basis[pl.ds(pl.multiple_of(pair * 128, 128), 128), :]
                r = dot_split(x, wt, NN)
                far_ref[2 * pair] = r[:8]
                far_ref[2 * pair + 1] = r[8:]
        return carry

    lax.fori_loop(0, leaves // 8, far_body, 0)
    keep.wait()
    for c in nears:
        c.wait_recv()
    for c in nears:
        c.wait_send()


def local(
    panels,
    near_tiles,
    near_cols,
    leaf_order,
    leaf_basis,
    local_mats,
    local_flags,
    cross_coupling,
    cross_transfer,
    cross_flags,
):
    rows = panels.shape[0]
    leaves, rank, size = leaf_basis.shape
    n_leaf = lax.axis_size("leaf")
    n_vec = lax.axis_size("vec")
    vmem = pl.BlockSpec(memory_space=pltpu.VMEM)
    smem = pl.BlockSpec(memory_space=pltpu.SMEM)
    hbm = pl.BlockSpec(memory_space=pl.ANY)
    ordered = pl.pallas_call(
        order_kernel,
        out_shape=jax.ShapeDtypeStruct((leaves, rows, size), f32),
        in_specs=[vmem, vmem],
        out_specs=vmem,
        name="order",
    )(panels, leaf_order)
    basis2 = leaf_basis.reshape(leaves * rank, size)
    mats2 = local_mats.reshape(local_mats.shape[1] * rank, 2 * rank)
    groups = leaves // n_vec
    dma = pltpu.SemaphoreType.DMA
    far, near = pl.pallas_call(
        functools.partial(main_kernel, n_leaf, n_vec),
        out_shape=(
            jax.ShapeDtypeStruct((leaves, rows, size), f32),
            jax.ShapeDtypeStruct((n_vec, groups, rows, size), f32),
        ),
        in_specs=[vmem, smem, smem, smem, vmem, vmem, hbm, hbm, hbm],
        out_specs=(vmem, vmem),
        scratch_shapes=[
            pltpu.VMEM(near_tiles.shape, f32),
            pltpu.VMEM(basis2.shape, f32),
            pltpu.VMEM(mats2.shape, f32),
            pltpu.VMEM((n_vec, leaves + 2 * W, rows, size), f32),
            pltpu.VMEM((leaves + 2 * W, 2 * n_vec * rows, size), bf16),
            pltpu.VMEM((leaves // 2, rows, size), f32),
            pltpu.VMEM((leaves // 2, rows, size), f32),
            pltpu.VMEM((n_leaf, rows, 2 * rank), f32),
            pltpu.VMEM((n_leaf, rows, 2 * rank), f32),
            pltpu.VMEM((n_vec, groups, rows, size), f32),
            dma((4,)),
            dma((n_vec,)),
            dma((n_vec,)),
            dma((2, n_vec)),
            dma((2, n_vec)),
            dma((n_leaf,)),
            dma((n_leaf,)),
            dma((n_vec,)),
            dma((n_vec,)),
        ],
        compiler_params=pltpu.CompilerParams(
            collective_id=0, has_side_effects=True, vmem_limit_bytes=40 * 1024 * 1024
        ),
        name="tree",
    )(
        ordered,
        near_cols,
        local_flags,
        cross_flags,
        cross_coupling,
        cross_transfer,
        near_tiles,
        basis2,
        mats2,
    )
    return pl.pallas_call(
        restore_kernel,
        out_shape=jax.ShapeDtypeStruct(panels.shape, f32),
        in_specs=[vmem, vmem, vmem],
        out_specs=vmem,
        name="restore",
    )(far, near, leaf_order)


def solution(mesh):
    return jax.shard_map(
        local,
        mesh=mesh,
        in_specs=(
            P("vec", "leaf"),
            P("leaf", None, "vec", None),
            P("leaf", None),
            P("leaf", None),
            P("leaf", None, None),
            P("leaf", None, None, None),
            P("leaf", None),
            P(),
            P(),
            P(),
        ),
        out_specs=P("vec", "leaf"),
        check_vma=False,
    )
```

time: 109 us -> 56.6 us (0.52)
  the two profiles are of different devices: /device:TPU:0 before, /device:TPU:1 now
where the time goes in v1:
time: 56.6 us; the launch traced here: 56.2 us
  Pallas kernels  44.6 us (79%)
  local copies, waits for them, and re-layouts  11.6 us (20%)
    pallas_call x1, Pallas kernels, local(): pl.pallas_call(functools.partial(main_kernel, n_leaf, n_vec), out_shape=(...  35.8 us
    unnamed x21, local copies, waits for them, and re-layouts  11.6 us
    pallas_call x1, Pallas kernels, local(): pl.pallas_call(restore_kernel, out_shape=jax.ShapeDtypeStruct(panels.shap...  5.41 us
    pallas_call x1, Pallas kernels, local(): pl.pallas_call(order_kernel, out_shape=jax.ShapeDtypeStruct((leaves, rows...  3.34 us

profile of v1, /device:TPU:1, one launch (start us, length us, event | category | flops | bytes accessed | tf_op | source)
XLA Modules:
  0.0 56.2 jit_solution(4054877667388046389)
XLA Ops:
  0.0 0.8 %copy.11.cols_ref = s32[64,4]{1,0:T(8,128)S(1)} copy(s32[64,4]{0,1:T(4,128)} %param.12) | data formatting | bytes 2048 | tf_op args[2]
  0.8 3.3 %order.1.own_ref = f32[64,8,128]{2,1,0:T(8,128)} custom-call(f32[8,8192]{1,0:T(8,128)} %panels_ref.1, s32[64,128]{1,0:T(8,128)} %order_ref.3), custom_call_target="tpu_custom_call" | custom-call | tf_op jit(solution)/shard_map/order/pallas_call | solution.py:423
  4.1 0.0 copy-start
  4.1 2.2 %copy-done = f32[64,4,32,128]{3,2,1,0:T(8,128)S(1)} copy-done((f32[64,4,32,128]{3,2,1,0:T(8,128)S(1)}, f32[64,4,32,128]{3,2,1,0:T(8,128)}, u32[]{:S(2)}) %copy-start) | copy-done | bytes 4194328
  6.3 0.0 copy-start.1
  6.3 1.6 %copy-done.1 = f32[64,64,128]{2,1,0:T(8,128)S(1)} copy-done((f32[64,64,128]{2,1,0:T(8,128)S(1)}, f32[64,64,128]{2,1,0:T(8,128)}, u32[]{:S(2)}) %copy-start.1) | copy-done | bytes 2097176
  7.9 0.0 copy-start.2
  7.9 1.6 %copy-done.2 = f32[1,63,64,128]{3,2,1,0:T(8,128)S(1)} copy-done((f32[1,63,64,128]{3,2,1,0:T(8,128)S(1)}, f32[1,63,64,128]{3,2,1,0:T(8,128)}, u32[]{:S(2)}) %copy-start.2) | copy-done | bytes 2064408
  9.5 0.0 copy-start.3
  9.5 0.9 %copy-done.3 = f32[64,8,128]{2,1,0:T(8,128)S(1)} copy-done((f32[64,8,128]{2,1,0:T(8,128)S(1)}, f32[64,8,128]{2,1,0:T(8,128)}, u32[]{:S(2)}) %copy-start.3) | copy-done | bytes 262168
  10.4 0.0 copy-start.6
  10.4 0.9 %copy-done.6 = f32[6,64,64]{2,1,0:T(8,128)S(1)} copy-done((f32[6,64,64]{2,1,0:T(8,128)S(1)}, f32[6,64,64]{2,1,0:T(8,128)}, u32[]{:S(2)}) %copy-start.6) | copy-done | bytes 98328
  11.4 0.0 copy-start.7
  11.4 0.9 %copy-done.7 = f32[4,64,64]{2,1,0:T(8,128)S(1)} copy-done((f32[4,64,64]{2,1,0:T(8,128)S(1)}, f32[4,64,64]{2,1,0:T(8,128)}, u32[]{:S(2)}) %copy-start.7) | copy-done | bytes 65560
  12.3 0.0 copy-start.8
  12.3 0.7 %copy-done.8 = s32[1,63]{1,0:T(1,128)S(1)} copy-done((s32[1,63]{1,0:T(1,128)S(1)}, s32[1,63]{1,0:T(1,128)}, u32[]{:S(2)}) %copy-start.8) | copy-done | bytes 276
  12.9 0.0 copy-start.9
  12.9 0.7 %copy-done.9 = s32[6]{0:T(128)S(1)} copy-done((s32[6]{0:T(128)S(1)}, s32[6]{0:T(128)}, u32[]{:S(2)}) %copy-start.9) | copy-done | bytes 48
  13.6 35.8 %tree.1 = (f32[64,8,128]{2,1,0:T(8,128)S(1)}, f32[4,16,8,128]{3,2,1,0:T(8,128)S(1)}) custom-call(f32[64,8,128]{2,1,0:T(8,128)S(1)} %copy-done.3, s32[64,4]{1,0:T(8,128)S(1)} %copy.11.cols_ref, s32[1,63]{1,0:T(1,128)S(1)} %copy-done.8, s32[6]{0:T(128)S(1)} %copy-done.9, f32[6,64,64]{2,1,0:T(8,128)S(1)} %copy-done.6, f32[4,64,64]{2,1,0:T(8,128)S(1)} %copy-done.7, ...), custom_call_target="tpu_custom_call" | custom-call | tf_op jit(solution)/shard_map/tree/pallas_call | solution.py:434
  49.4 0.0 copy-start.4
  49.4 0.7 %copy-done.4 = f32[64,8,128]{2,1,0:T(8,128)} copy-done((f32[64,8,128]{2,1,0:T(8,128)}, f32[64,8,128]{2,1,0:T(8,128)S(1)}, u32[]{:S(2)}) %copy-start.4) | copy-done | bytes 262168
  50.1 0.0 copy-start.5
  50.1 0.7 %copy-done.5 = f32[4,16,8,128]{3,2,1,0:T(8,128)} copy-done((f32[4,16,8,128]{3,2,1,0:T(8,128)}, f32[4,16,8,128]{3,2,1,0:T(8,128)S(1)}, u32[]{:S(2)}) %copy-start.5) | copy-done | bytes 262168
  50.8 5.4 %restore.1 = f32[8,8192]{1,0:T(8,128)} custom-call(f32[64,8,128]{2,1,0:T(8,128)} %copy-done.4, f32[4,16,8,128]{3,2,1,0:T(8,128)} %copy-done.5, s32[64,128]{1,0:T(8,128)} %order_ref.3), custom_call_target="tpu_custom_call" | custom-call | tf_op jit(solution)/shard_map/restore/pallas_call | solution.py:478
Async XLA Ops:
  4.1 2.2 %copy-start = (f32[64,4,32,128]{3,2,1,0:T(8,128)S(1)}, f32[64,4,32,128]{3,2,1,0:T(8,128)}, u32[]{:S(2)}) copy-start(f32[64,4,32,128]{3,2,1,0:T(8,128)} %tiles_hbm.1) | copy-start | bytes 12582916
  6.3 1.6 %copy-start.1 = (f32[64,64,128]{2,1,0:T(8,128)S(1)}, f32[64,64,128]{2,1,0:T(8,128)}, u32[]{:S(2)}) copy-start(f32[64,64,128]{2,1,0:T(8,128)} %param.14) | copy-start | bytes 6291460
  7.9 1.6 %copy-start.2 = (f32[1,63,64,128]{3,2,1,0:T(8,128)S(1)}, f32[1,63,64,128]{3,2,1,0:T(8,128)}, u32[]{:S(2)}) copy-start(f32[1,63,64,128]{3,2,1,0:T(8,128)} %param.15) | copy-start | bytes 6193156
  9.5 0.9 %copy-start.3 = (f32[64,8,128]{2,1,0:T(8,128)S(1)}, f32[64,8,128]{2,1,0:T(8,128)}, u32[]{:S(2)}) copy-start(f32[64,8,128]{2,1,0:T(8,128)} %order.1.own_ref) | copy-start | bytes 786436
  10.4 0.9 %copy-start.6 = (f32[6,64,64]{2,1,0:T(8,128)S(1)}, f32[6,64,64]{2,1,0:T(8,128)}, u32[]{:S(2)}) copy-start(f32[6,64,64]{2,1,0:T(8,128)} %cross_c_ref.1) | copy-start | bytes 294916
  11.4 0.9 %copy-start.7 = (f32[4,64,64]{2,1,0:T(8,128)S(1)}, f32[4,64,64]{2,1,0:T(8,128)}, u32[]{:S(2)}) copy-start(f32[4,64,64]{2,1,0:T(8,128)} %cross_e_ref.1) | copy-start | bytes 196612
  12.3 0.7 %copy-start.8 = (s32[1,63]{1,0:T(1,128)S(1)}, s32[1,63]{1,0:T(1,128)}, u32[]{:S(2)}) copy-start(s32[1,63]{1,0:T(1,128)} %flags_ref.1) | copy-start | bytes 760
  12.9 0.7 %copy-start.9 = (s32[6]{0:T(128)S(1)}, s32[6]{0:T(128)}, u32[]{:S(2)}) copy-start(s32[6]{0:T(128)} %cross_flags_ref.1) | copy-start | bytes 76
  49.4 0.7 %copy-start.4 = (f32[64,8,128]{2,1,0:T(8,128)}, f32[64,8,128]{2,1,0:T(8,128)S(1)}, u32[]{:S(2)}) copy-start(f32[64,8,128]{2,1,0:T(8,128)S(1)} %get-tuple-element.7.far_ref) | copy-start | bytes 786436
  50.1 0.7 %copy-start.5 = (f32[4,16,8,128]{3,2,1,0:T(8,128)}, f32[4,16,8,128]{3,2,1,0:T(8,128)S(1)}, u32[]{:S(2)}) copy-start(f32[4,16,8,128]{3,2,1,0:T(8,128)S(1)} %get-tuple-element.8.near_ref) | copy-start | bytes 786436

commit v2 on v1

--- a/solution.py
+++ b/solution.py
@@ -50,18 +50,16 @@
     def body(i, carry):
         for u in range(span):
             leaf = i * span + u
-            hot = hot_of(order_ref[pl.ds(leaf, 1), :])
-            x = stacked(panels_ref[:, pl.ds(pl.multiple_of(leaf * size, size), size)])
-            r = lax.dot_general(x, hot, NN, preferred_element_type=f32)
-            rows = panels_ref.shape[0]
-            out_ref[leaf] = r[:rows] + r[rows:]
+            x = panels_ref[:, pl.ds(pl.multiple_of(leaf * size, size), size)]
+            spots = jnp.broadcast_to(order_ref[pl.ds(leaf, 1), :], x.shape)
+            out_ref[leaf] = jnp.take_along_axis(x, spots, axis=1)
         return carry
 
     lax.fori_loop(0, leaves // span, body, 0)
 
 
-def restore_kernel(far_ref, near_ref, order_ref, out_ref):
-    leaves, size = order_ref.shape
+def restore_kernel(far_ref, near_ref, inverse_ref, out_ref):
+    leaves, _, size = far_ref.shape
     n_vec = near_ref.shape[0]
     piece = size // n_vec
     rows = out_ref.shape[0]
@@ -77,9 +75,10 @@
                 moved = parts[v] if shift == 0 else pltpu.roll(parts[v], shift, 1)
                 near = jnp.where(block == v, moved, near)
             combined = near + far_ref[leaf]
-            hot = hot_of(order_ref[pl.ds(leaf, 1), :])
-            r = lax.dot_general(stacked(combined), hot, NT, preferred_element_type=f32)
-            out_ref[:, pl.ds(pl.multiple_of(leaf * size, size), size)] = r[:rows] + r[rows:]
+            spots = inverse_ref[leaf].astype(jnp.int32)
+            out_ref[:, pl.ds(pl.multiple_of(leaf * size, size), size)] = jnp.take_along_axis(
+                combined, spots, axis=1
+            )
         return carry
 
     lax.fori_loop(0, leaves // n_vec, body, 0)
@@ -89,16 +88,23 @@
     n_leaf,
     n_vec,
     own_ref,
+    order_ref,
+    cols_hbm,
+    flags_hbm,
+    cross_flags_hbm,
+    cross_c_hbm,
+    cross_e_hbm,
+    tiles_hbm,
+    basis_hbm,
+    mats_hbm,
+    far_ref,
+    near_ref,
+    inverse_ref,
     cols_ref,
     flags_ref,
     cross_flags_ref,
     cross_c_ref,
     cross_e_ref,
-    tiles_hbm,
-    basis_hbm,
-    mats_hbm,
-    far_ref,
-    near_ref,
     tiles,
     basis,
     mats,
@@ -131,6 +137,20 @@
     load_m.start()
     load_t.start()
     load_o.start()
+    small = [
+        pltpu.make_async_copy(src, dst, load_sem.at[4 + i])
+        for i, (src, dst) in enumerate(
+            [
+                (cols_hbm, cols_ref),
+                (flags_hbm, flags_ref),
+                (cross_flags_hbm, cross_flags_ref),
+                (cross_c_hbm, cross_c_ref),
+                (cross_e_hbm, cross_e_ref),
+            ]
+        )
+    ]
+    for c in small:
+        c.start()
 
     right = lax.rem(li + 1, n_leaf)
     left = lax.rem(li + n_leaf - 1, n_leaf)
@@ -154,13 +174,17 @@
         greeted += 1
     pl.semaphore_wait(barrier, greeted)
 
-    def gather_copy(d):
+    beside = vi + 1 - 2 * lax.rem(vi, 2)
+    across = lax.rem(vi + 2, n_vec)
+
+    def gather_copy(kind):
+        block = ext.at[across if kind == 2 else vi, pl.ds(W, leaves)]
         return pltpu.make_async_remote_copy(
-            src_ref=own_ref,
-            dst_ref=ext.at[vi, pl.ds(W, leaves)],
-            send_sem=gs_send.at[d],
-            recv_sem=gs_recv.at[n_vec - d],
-            device_id=(li, lax.rem(vi + d, n_vec)),
+            src_ref=block if kind == 2 else own_ref,
+            dst_ref=block,
+            send_sem=gs_send.at[kind],
+            recv_sem=gs_recv.at[kind],
+            device_id=(li, across if kind == 0 else beside),
             device_id_type=MESH,
         )
 
@@ -176,9 +200,10 @@
             device_id_type=MESH,
         )
 
-    gathers = [gather_copy(d) for d in range(1, n_vec)]
+    assert n_vec == 4
+    gathers = [gather_copy(kind) for kind in range(3)]
     halos = [halo_copy(side, d) for side in range(2) for d in range(n_vec)]
-    for c in halos + gathers:
+    for c in gathers[:2] + halos:
         c.start()
 
     lane = lax.broadcasted_iota(jnp.int32, (8, 2 * rank), 1)
@@ -254,9 +279,23 @@
     for c in pays:
         c.start()
 
+    gathers[0].wait_recv()
+    gathers[2].start()
+    counts = lax.broadcasted_iota(jnp.int32, (8, 128), 1).astype(f32).astype(bf16)
+
+    def inverse_body(i, carry):
+        for w in range(8):
+            leaf = i * 8 + w
+            hot = hot_of(order_ref[pl.ds(leaf, 1), :])
+            inverse_ref[leaf] = lax.dot_general(counts, hot, NT, preferred_element_type=f32)
+        return carry
+
+    lax.fori_loop(0, leaves // 8, inverse_body, 0)
     load_o.wait()
     load_t.wait()
-    for c in halos + gathers:
+    for c in small:
+        c.wait()
+    for c in halos + gathers[1:]:
         c.wait_recv()
     for c in halos + gathers:
         c.wait_send()
@@ -273,7 +312,7 @@
     piece = tiles.shape[2]
 
     def place(leaf, n):
-        return jnp.clip(cols_ref[leaf, n] - base, 0, leaves + 2 * W - 1)
+        return jnp.clip(cols_ref[n, leaf] - base, 0, leaves + 2 * W - 1)
 
     def near_body(g, carry):
         outs = []
@@ -418,7 +457,6 @@
     n_leaf = lax.axis_size("leaf")
     n_vec = lax.axis_size("vec")
     vmem = pl.BlockSpec(memory_space=pltpu.VMEM)
-    smem = pl.BlockSpec(memory_space=pltpu.SMEM)
     hbm = pl.BlockSpec(memory_space=pl.ANY)
     ordered = pl.pallas_call(
         order_kernel,
@@ -431,15 +469,21 @@
     mats2 = local_mats.reshape(local_mats.shape[1] * rank, 2 * rank)
     groups = leaves // n_vec
     dma = pltpu.SemaphoreType.DMA
-    far, near = pl.pallas_call(
+    far, near, inverse = pl.pallas_call(
         functools.partial(main_kernel, n_leaf, n_vec),
         out_shape=(
             jax.ShapeDtypeStruct((leaves, rows, size), f32),
             jax.ShapeDtypeStruct((n_vec, groups, rows, size), f32),
+            jax.ShapeDtypeStruct((leaves, rows, size), f32),
         ),
-        in_specs=[vmem, smem, smem, smem, vmem, vmem, hbm, hbm, hbm],
-        out_specs=(vmem, vmem),
+        in_specs=[vmem, vmem] + [hbm] * 8,
+        out_specs=(vmem, vmem, vmem),
         scratch_shapes=[
+            pltpu.SMEM(near_cols.shape[::-1], jnp.int32),
+            pltpu.SMEM(local_flags.shape, jnp.int32),
+            pltpu.SMEM(cross_flags.shape, jnp.int32),
+            pltpu.VMEM(cross_coupling.shape, f32),
+            pltpu.VMEM(cross_transfer.shape, f32),
             pltpu.VMEM(near_tiles.shape, f32),
             pltpu.VMEM(basis2.shape, f32),
             pltpu.VMEM(mats2.shape, f32),
@@ -450,7 +494,7 @@
             pltpu.VMEM((n_leaf, rows, 2 * rank), f32),
             pltpu.VMEM((n_leaf, rows, 2 * rank), f32),
             pltpu.VMEM((n_vec, groups, rows, size), f32),
-            dma((4,)),
+            dma((9,)),
             dma((n_vec,)),
             dma((n_vec,)),
             dma((2, n_vec)),
@@ -461,12 +505,13 @@
             dma((n_vec,)),
         ],
         compiler_params=pltpu.CompilerParams(
-            collective_id=0, has_side_effects=True, vmem_limit_bytes=40 * 1024 * 1024
+            collective_id=0, has_side_effects=True, vmem_limit_bytes=61 * 1024 * 1024
         ),
         name="tree",
     )(
         ordered,
-        near_cols,
+        leaf_order,
+        near_cols.T,
         local_flags,
         cross_flags,
         cross_coupling,
@@ -481,7 +526,7 @@
         in_specs=[vmem, vmem, vmem],
         out_specs=vmem,
         name="restore",
-    )(far, near, leaf_order)
+    )(far, near, inverse)
 
 
 def solution(mesh):

time: 56.6 us -> 39.7 us (0.70)
  the two profiles are of different devices: /device:TPU:1 before, /device:TPU:0 now
where the time goes in v2:
time: 39.7 us; the launch traced here: 39.5 us
  Pallas kernels  39.5 us (99%)
    pallas_call x1, Pallas kernels, local(): pl.pallas_call(functools.partial(main_kernel, n_leaf, n_vec), out_shape=(...  32.9 us
    pallas_call x1, Pallas kernels, local(): pl.pallas_call(restore_kernel, out_shape=jax.ShapeDtypeStruct(panels.shap...  4.26 us
    pallas_call x1, Pallas kernels, local(): pl.pallas_call(order_kernel, out_shape=jax.ShapeDtypeStruct((leaves, rows...  2.37 us

profile of v2, /device:TPU:0, one launch (start us, length us, event | category | flops | bytes accessed | tf_op | source)
XLA Modules:
  0.0 39.5 jit_solution(10207031880196736197)
XLA Ops:
  0.0 2.4 %order.1.own_ref = f32[64,8,128]{2,1,0:T(8,128)} custom-call(f32[8,8192]{1,0:T(8,128)} %panels_ref.1, s32[64,128]{1,0:T(8,128)} %order_ref.3), custom_call_target="tpu_custom_call" | custom-call | tf_op jit(solution)/shard_map/order/pallas_call | solution.py:461
  2.4 32.9 %tree.1 = (f32[64,8,128]{2,1,0:T(8,128)}, f32[4,16,8,128]{3,2,1,0:T(8,128)}, f32[64,8,128]{2,1,0:T(8,128)}) custom-call(f32[64,8,128]{2,1,0:T(8,128)} %order.1.own_ref, s32[64,128]{1,0:T(8,128)} %order_ref.3, s32[4,64]{1,0:T(4,128)} %bitcast.5, s32[1,63]{1,0:T(1,128)} %flags_hbm.1, s32[6]{0:T(128)} %cross_flags_hbm.1, f32[6,64,64]{2,1,0:T(8,128)} %cross_c_hbm.1, ...), custom_call_target="tpu_custom_call" | custom-call | tf_op jit(solution)/shard_map/tree/pallas_call | solution.py:472
  35.2 4.3 %restore.1 = f32[8,8192]{1,0:T(8,128)} custom-call(f32[64,8,128]{2,1,0:T(8,128)} %get-tuple-element.8.far_ref, f32[4,16,8,128]{3,2,1,0:T(8,128)} %get-tuple-element.9.near_ref, f32[64,8,128]{2,1,0:T(8,128)} %get-tuple-element.10.inverse_ref), custom_call_target="tpu_custom_call" | custom-call | tf_op jit(solution)/shard_map/restore/pallas_call | solution.py:523

commit v3 on v2

--- a/solution.py
+++ b/solution.py
@@ -161,13 +161,7 @@
             barrier, inc=1, device_id=(li, lax.rem(vi + d, n_vec)), device_id_type=MESH
         )
         greeted += 1
-    for side in (left, right):
-        for u in range(n_vec):
-            pl.semaphore_signal(
-                barrier, inc=1, device_id=(side, lax.rem(vi + u, n_vec)), device_id_type=MESH
-            )
-            greeted += 1
-    for d in range(2, n_leaf - 1):
+    for d in range(1, n_leaf):
         pl.semaphore_signal(
             barrier, inc=1, device_id=(lax.rem(li + d, n_leaf), vi), device_id_type=MESH
         )
@@ -188,22 +182,34 @@
             device_id_type=MESH,
         )
 
-    def halo_copy(side, d):
-        start = leaves - W if side == 0 else 0
-        to = 0 if side == 0 else leaves + W
+    rims = (0, leaves + W)
+
+    def halo_copy(side):
         return pltpu.make_async_remote_copy(
-            src_ref=own_ref.at[pl.ds(start, W)],
-            dst_ref=ext.at[vi, pl.ds(to, W)],
-            send_sem=halo_send.at[side, d],
-            recv_sem=halo_recv.at[side, (n_vec - d) % n_vec],
-            device_id=(right if side == 0 else left, lax.rem(vi + d, n_vec)),
+            src_ref=own_ref.at[pl.ds(leaves - W if side == 0 else 0, W)],
+            dst_ref=ext.at[vi, pl.ds(rims[side], W)],
+            send_sem=halo_send.at[side, 3],
+            recv_sem=halo_recv.at[side, 3],
+            device_id=(right if side == 0 else left, vi),
+            device_id_type=MESH,
+        )
+
+    def rim_copy(side, kind):
+        block = ext.at[across if kind == 2 else vi, pl.ds(rims[side], W)]
+        return pltpu.make_async_remote_copy(
+            src_ref=block,
+            dst_ref=block,
+            send_sem=halo_send.at[side, kind],
+            recv_sem=halo_recv.at[side, kind],
+            device_id=(li, across if kind == 0 else beside),
             device_id_type=MESH,
         )
 
     assert n_vec == 4
     gathers = [gather_copy(kind) for kind in range(3)]
-    halos = [halo_copy(side, d) for side in range(2) for d in range(n_vec)]
-    for c in gathers[:2] + halos:
+    halos = [halo_copy(side) for side in range(2)]
+    rim_copies = [[rim_copy(side, kind) for side in range(2)] for kind in range(3)]
+    for c in halos + gathers[:2]:
         c.start()
 
     lane = lax.broadcasted_iota(jnp.int32, (8, 2 * rank), 1)
@@ -230,6 +236,10 @@
         return carry
 
     lax.fori_loop(0, leaves // 8, skel_body, 0)
+    for c in halos:
+        c.wait_recv()
+    for c in rim_copies[0] + rim_copies[1]:
+        c.start()
     load_m.wait()
 
     def mat_pair(q):
@@ -279,8 +289,6 @@
     for c in pays:
         c.start()
 
-    gathers[0].wait_recv()
-    gathers[2].start()
     counts = lax.broadcasted_iota(jnp.int32, (8, 128), 1).astype(f32).astype(bf16)
 
     def inverse_body(i, carry):
@@ -291,61 +299,14 @@
         return carry
 
     lax.fori_loop(0, leaves // 8, inverse_body, 0)
-    load_o.wait()
-    load_t.wait()
+    for c in rim_copies[0]:
+        c.wait_recv()
+    for c in rim_copies[2]:
+        c.start()
+    gathers[0].wait_recv()
+    gathers[2].start()
     for c in small:
         c.wait()
-    for c in halos + gathers[1:]:
-        c.wait_recv()
-    for c in halos + gathers:
-        c.wait_send()
-
-    def split_body(i, carry):
-        for w in range(4):
-            e = i * 4 + w
-            xs[e] = stacked(ext[:, e].reshape(n_vec * 8, 128))
-        return carry
-
-    lax.fori_loop(0, (leaves + 2 * W) // 4, split_body, 0)
-    base = li * leaves - W
-    slots = tiles.shape[1]
-    piece = tiles.shape[2]
-
-    def place(leaf, n):
-        return jnp.clip(cols_ref[n, leaf] - base, 0, leaves + 2 * W - 1)
-
-    def near_body(g, carry):
-        outs = []
-        for w in range(n_vec):
-            leaf = g * n_vec + w
-            x = jnp.concatenate([xs[place(leaf, n)] for n in range(slots)], axis=1)
-            t = jnp.concatenate([stacked(tiles[leaf, n]) for n in range(slots)], axis=1)
-            r = lax.dot_general(x, t, NT, preferred_element_type=f32)
-            half = r.shape[0] // 2
-            r = r[:half] + r[half:]
-            outs.append(r[:, :piece] + r[:, piece:])
-        nout[:, g] = jnp.concatenate(outs, axis=1).reshape(n_vec, 8, n_vec * piece)
-        return carry
-
-    lax.fori_loop(0, leaves // n_vec, near_body, 0)
-
-    def near_copy(d):
-        u = lax.rem(vi + d, n_vec)
-        return pltpu.make_async_remote_copy(
-            src_ref=nout.at[u],
-            dst_ref=near_ref.at[vi],
-            send_sem=near_send.at[d],
-            recv_sem=near_recv.at[n_vec - d],
-            device_id=(li, u),
-            device_id_type=MESH,
-        )
-
-    nears = [near_copy(d) for d in range(1, n_vec)]
-    for c in nears:
-        c.start()
-    keep = pltpu.make_async_copy(nout.at[vi], near_ref.at[vi], near_send.at[0])
-    keep.start()
-
     for c in pays:
         c.wait_recv()
     for c in pays:
@@ -413,6 +374,64 @@
         else:
             for t in range(half):
                 down_one(t)
+
+    load_o.wait()
+    load_t.wait()
+    for c in gathers[1:] + rim_copies[1] + rim_copies[2]:
+        c.wait_recv()
+    for c in halos + gathers + rim_copies[0] + rim_copies[1] + rim_copies[2]:
+        c.wait_send()
+
+    def split_body(i, carry):
+        for w in range(4):
+            e = i * 4 + w
+            xs[e] = stacked(ext[:, e].reshape(n_vec * 8, 128))
+        return carry
+
+    lax.fori_loop(0, (leaves + 2 * W) // 4, split_body, 0)
+    base = li * leaves - W
+    slots = tiles.shape[1]
+    piece = tiles.shape[2]
+
+    def place(leaf, n):
+        return jnp.clip(cols_ref[n, leaf] - base, 0, leaves + 2 * W - 1)
+
+    def near_body(g, carry):
+        outs = []
+        for w in range(n_vec):
+            leaf = g * n_vec + w
+            x = jnp.concatenate([xs[place(leaf, n)] for n in range(slots)], axis=1)
+            t = jnp.concatenate([stacked(tiles[leaf, n]) for n in range(slots)], axis=1)
+            r = lax.dot_general(x, t, NT, preferred_element_type=f32)
+            half = r.shape[0] // 2
+            r = r[:half] + r[half:]
+            outs.append(r[:, :piece] + r[:, piece:])
+        nout[:, g] = jnp.concatenate(outs, axis=1).reshape(n_vec, 8, n_vec * piece)
+        return carry
+
+    half_groups = leaves // n_vec // 2
+
+    def near_copy(d, part):
+        u = lax.rem(vi + d, n_vec)
+        span = pl.ds(part * half_groups, half_groups)
+        return pltpu.make_async_remote_copy(
+            src_ref=nout.at[u, span],
+            dst_ref=near_ref.at[vi, span],
+            send_sem=near_send.at[part, d],
+            recv_sem=near_recv.at[part, n_vec - d],
+            device_id=(li, u),
+            device_id_type=MESH,
+        )
+
+    nears = []
+    for part in range(2):
+        lax.fori_loop(part * half_groups, (part + 1) * half_groups, near_body, 0)
+        batch = [near_copy(d, part) for d in (2, 1, 3)]
+        for c in batch:
+            c.start()
+        nears += batch
+    keep = pltpu.make_async_copy(nout.at[vi], near_ref.at[vi], near_send.at[0, 0])
+    keep.start()
 
     def far_body(i, carry):
         for w in range(2):
@@ -501,8 +520,8 @@
             dma((2, n_vec)),
             dma((n_leaf,)),
             dma((n_leaf,)),
-            dma((n_vec,)),
-            dma((n_vec,)),
+            dma((2, n_vec)),
+            dma((2, n_vec)),
         ],
         compiler_params=pltpu.CompilerParams(
             collective_id=0, has_side_effects=True, vmem_limit_bytes=61 * 1024 * 1024

time: 39.7 us -> 39.2 us (0.987)
  Pallas kernels: 39.5 us -> 39 us
    pallas_call x1, Pallas kernels: 32.9 us -> 32.4 us  [local(): pl.pallas_call(functools.partial(main_kernel, n_leaf, n_vec), out_shape=(...]
where the time goes in v3:
time: 39.2 us; the launch traced here: 39 us
  Pallas kernels  39 us (99%)
    pallas_call x1, Pallas kernels, local(): pl.pallas_call(functools.partial(main_kernel, n_leaf, n_vec), out_shape=(...  32.4 us
    pallas_call x1, Pallas kernels, local(): pl.pallas_call(restore_kernel, out_shape=jax.ShapeDtypeStruct(panels.shap...  4.26 us
    pallas_call x1, Pallas kernels, local(): pl.pallas_call(order_kernel, out_shape=jax.ShapeDtypeStruct((leaves, rows...  2.37 us

profile of v3, /device:TPU:0, one launch (start us, length us, event | category | flops | bytes accessed | tf_op | source)
XLA Modules:
  0.0 39.0 jit_solution(14087672244988454916)
XLA Ops:
  0.0 2.4 %order.1.own_ref = f32[64,8,128]{2,1,0:T(8,128)} custom-call(f32[8,8192]{1,0:T(8,128)} %panels_ref.1, s32[64,128]{1,0:T(8,128)} %order_ref.3), custom_call_target="tpu_custom_call" | custom-call | tf_op jit(solution)/shard_map/order/pallas_call | solution.py:480
  2.4 32.4 %tree.1 = (f32[64,8,128]{2,1,0:T(8,128)}, f32[4,16,8,128]{3,2,1,0:T(8,128)}, f32[64,8,128]{2,1,0:T(8,128)}) custom-call(f32[64,8,128]{2,1,0:T(8,128)} %order.1.own_ref, s32[64,128]{1,0:T(8,128)} %order_ref.3, s32[4,64]{1,0:T(4,128)} %bitcast.5, s32[1,63]{1,0:T(1,128)} %flags_hbm.1, s32[6]{0:T(128)} %cross_flags_hbm.1, f32[6,64,64]{2,1,0:T(8,128)} %cross_c_hbm.1, ...), custom_call_target="tpu_custom_call" | custom-call | tf_op jit(solution)/shard_map/tree/pallas_call | solution.py:491
  34.8 4.3 %restore.1 = f32[8,8192]{1,0:T(8,128)} custom-call(f32[64,8,128]{2,1,0:T(8,128)} %get-tuple-element.8.far_ref, f32[4,16,8,128]{3,2,1,0:T(8,128)} %get-tuple-element.9.near_ref, f32[64,8,128]{2,1,0:T(8,128)} %get-tuple-element.10.inverse_ref), custom_call_target="tpu_custom_call" | custom-call | tf_op jit(solution)/shard_map/restore/pallas_call | solution.py:542

commit v4 on v3

--- a/solution.py
+++ b/solution.py
@@ -45,7 +45,7 @@
 
 def order_kernel(panels_ref, order_ref, out_ref):
     leaves, size = order_ref.shape
-    span = 8
+    span = 32
 
     def body(i, carry):
         for u in range(span):
@@ -65,7 +65,7 @@
     rows = out_ref.shape[0]
     block = lax.broadcasted_iota(jnp.int32, (rows, size), 1) // piece
 
-    def body(g, carry):
+    def group(g):
         parts = [near_ref[v, g] for v in range(n_vec)]
         for u in range(n_vec):
             leaf = g * n_vec + u
@@ -79,9 +79,13 @@
             out_ref[:, pl.ds(pl.multiple_of(leaf * size, size), size)] = jnp.take_along_axis(
                 combined, spots, axis=1
             )
-        return carry
-
-    lax.fori_loop(0, leaves // n_vec, body, 0)
+
+    def body(i, carry):
+        for w in range(4):
+            group(i * 4 + w)
+        return carry
+
+    lax.fori_loop(0, leaves // n_vec // 4, body, 0)
 
 
 def main_kernel(
@@ -221,8 +225,8 @@
     load_b.wait()
 
     def skel_body(i, carry):
-        for w in range(2):
-            t = i * 2 + w
+        for w in range(4):
+            t = i * 4 + w
             sums = []
             for u in range(2):
                 pair = t * 2 + u
@@ -235,7 +239,7 @@
             hp[t] = jnp.where(low, even, odd) * root_half
         return carry
 
-    lax.fori_loop(0, leaves // 8, skel_body, 0)
+    lax.fori_loop(0, leaves // 16, skel_body, 0)
     for c in halos:
         c.wait_recv()
     for c in rim_copies[0] + rim_copies[1]:
@@ -258,7 +262,7 @@
         off += pairs
         pairs //= 2
     for (a, count), (b, half) in zip(offs[:-1], offs[1:]):
-        if half > 4:
+        if half > 8:
             def up_body(i, carry, a=a, b=b):
                 for w in range(4):
                     up(a, b, i * 4 + w)
@@ -292,13 +296,13 @@
     counts = lax.broadcasted_iota(jnp.int32, (8, 128), 1).astype(f32).astype(bf16)
 
     def inverse_body(i, carry):
-        for w in range(8):
-            leaf = i * 8 + w
+        for w in range(16):
+            leaf = i * 16 + w
             hot = hot_of(order_ref[pl.ds(leaf, 1), :])
             inverse_ref[leaf] = lax.dot_general(counts, hot, NT, preferred_element_type=f32)
         return carry
 
-    lax.fori_loop(0, leaves // 8, inverse_body, 0)
+    lax.fori_loop(0, leaves // 16, inverse_body, 0)
     for c in rim_copies[0]:
         c.wait_recv()
     for c in rim_copies[2]:
@@ -364,7 +368,7 @@
             down(a + 2 * t, swap(p))
             down(a + 2 * t + 1, p)
 
-        if half > 4:
+        if half > 8:
             def down_body(i, carry, down_one=down_one):
                 for w in range(4):
                     down_one(i * 4 + w)
@@ -396,7 +400,7 @@
     def place(leaf, n):
         return jnp.clip(cols_ref[n, leaf] - base, 0, leaves + 2 * W - 1)
 
-    def near_body(g, carry):
+    def near_group(g):
         outs = []
         for w in range(n_vec):
             leaf = g * n_vec + w
@@ -407,6 +411,10 @@
             r = r[:half] + r[half:]
             outs.append(r[:, :piece] + r[:, piece:])
         nout[:, g] = jnp.concatenate(outs, axis=1).reshape(n_vec, 8, n_vec * piece)
+
+    def near_body(i, carry):
+        for w in range(2):
+            near_group(i * 2 + w)
         return carry
 
     half_groups = leaves // n_vec // 2
@@ -425,7 +433,7 @@
 
     nears = []
     for part in range(2):
-        lax.fori_loop(part * half_groups, (part + 1) * half_groups, near_body, 0)
+        lax.fori_loop(part * half_groups // 2, (part + 1) * half_groups // 2, near_body, 0)
         batch = [near_copy(d, part) for d in (2, 1, 3)]
         for c in batch:
             c.start()
@@ -434,8 +442,8 @@
     keep.start()
 
     def far_body(i, carry):
-        for w in range(2):
-            t = i * 2 + w
+        for w in range(4):
+            t = i * 4 + w
             p = zp[t]
             s = swap(p)
             zero = jnp.zeros_like(p)
@@ -451,7 +459,7 @@
                 far_ref[2 * pair + 1] = r[8:]
         return carry
 
-    lax.fori_loop(0, leaves // 8, far_body, 0)
+    lax.fori_loop(0, leaves // 16, far_body, 0)
     keep.wait()
     for c in nears:
         c.wait_recv()

time: 39.2 us -> 32.2 us (0.82)
  Pallas kernels: 39 us -> 32 us
    pallas_call x1, Pallas kernels: 32.4 us -> 27.5 us  [local(): pl.pallas_call(functools.partial(main_kernel, n_leaf, n_vec), out_shape=(...]
    pallas_call x1, Pallas kernels: 4.26 us -> 2.59 us  [local(): pl.pallas_call(restore_kernel, out_shape=jax.ShapeDtypeStruct(panels.shap...]
    pallas_call x1, Pallas kernels: 2.37 us -> 1.97 us  [local(): pl.pallas_call(order_kernel, out_shape=jax.ShapeDtypeStruct((leaves, rows...]
where the time goes in v4:
time: 32.2 us; the launch traced here: 32 us
  Pallas kernels  32 us (99%)
    pallas_call x1, Pallas kernels, local(): pl.pallas_call(functools.partial(main_kernel, n_leaf, n_vec), out_shape=(...  27.5 us
    pallas_call x1, Pallas kernels, local(): pl.pallas_call(restore_kernel, out_shape=jax.ShapeDtypeStruct(panels.shap...  2.59 us
    pallas_call x1, Pallas kernels, local(): pl.pallas_call(order_kernel, out_shape=jax.ShapeDtypeStruct((leaves, rows...  1.97 us

profile of v4, /device:TPU:0, one launch (start us, length us, event | category | flops | bytes accessed | tf_op | source)
XLA Modules:
  0.0 32.0 jit_solution(615329460982655189)
XLA Ops:
  0.0 2.0 %order.1.own_ref = f32[64,8,128]{2,1,0:T(8,128)} custom-call(f32[8,8192]{1,0:T(8,128)} %panels_ref.1, s32[64,128]{1,0:T(8,128)} %order_ref.3), custom_call_target="tpu_custom_call" | custom-call | tf_op jit(solution)/shard_map/order/pallas_call | solution.py:488
  2.0 27.5 %tree.1 = (f32[64,8,128]{2,1,0:T(8,128)}, f32[4,16,8,128]{3,2,1,0:T(8,128)}, f32[64,8,128]{2,1,0:T(8,128)}) custom-call(f32[64,8,128]{2,1,0:T(8,128)} %order.1.own_ref, s32[64,128]{1,0:T(8,128)} %order_ref.3, s32[4,64]{1,0:T(4,128)} %bitcast.5, s32[1,63]{1,0:T(1,128)} %flags_hbm.1, s32[6]{0:T(128)} %cross_flags_hbm.1, f32[6,64,64]{2,1,0:T(8,128)} %cross_c_hbm.1, ...), custom_call_target="tpu_custom_call" | custom-call | tf_op jit(solution)/shard_map/tree/pallas_call | solution.py:499
  29.4 2.6 %restore.1 = f32[8,8192]{1,0:T(8,128)} custom-call(f32[64,8,128]{2,1,0:T(8,128)} %get-tuple-element.8.far_ref, f32[4,16,8,128]{3,2,1,0:T(8,128)} %get-tuple-element.9.near_ref, f32[64,8,128]{2,1,0:T(8,128)} %get-tuple-element.10.inverse_ref), custom_call_target="tpu_custom_call" | custom-call | tf_op jit(solution)/shard_map/restore/pallas_call | solution.py:550

commit v5 on v4

--- a/solution.py
+++ b/solution.py
@@ -81,11 +81,11 @@
             )
 
     def body(i, carry):
-        for w in range(4):
-            group(i * 4 + w)
-        return carry
-
-    lax.fori_loop(0, leaves // n_vec // 4, body, 0)
+        for w in range(8):
+            group(i * 8 + w)
+        return carry
+
+    lax.fori_loop(0, leaves // n_vec // 8, body, 0)
 
 
 def main_kernel(
@@ -225,8 +225,8 @@
     load_b.wait()
 
     def skel_body(i, carry):
-        for w in range(4):
-            t = i * 4 + w
+        for w in range(8):
+            t = i * 8 + w
             sums = []
             for u in range(2):
                 pair = t * 2 + u
@@ -239,7 +239,7 @@
             hp[t] = jnp.where(low, even, odd) * root_half
         return carry
 
-    lax.fori_loop(0, leaves // 16, skel_body, 0)
+    lax.fori_loop(0, leaves // 32, skel_body, 0)
     for c in halos:
         c.wait_recv()
     for c in rim_copies[0] + rim_copies[1]:
@@ -413,8 +413,8 @@
         nout[:, g] = jnp.concatenate(outs, axis=1).reshape(n_vec, 8, n_vec * piece)
 
     def near_body(i, carry):
-        for w in range(2):
-            near_group(i * 2 + w)
+        for w in range(4):
+            near_group(i * 4 + w)
         return carry
 
     half_groups = leaves // n_vec // 2
@@ -433,7 +433,7 @@
 
     nears = []
     for part in range(2):
-        lax.fori_loop(part * half_groups // 2, (part + 1) * half_groups // 2, near_body, 0)
+        lax.fori_loop(part * half_groups // 4, (part + 1) * half_groups // 4, near_body, 0)
         batch = [near_copy(d, part) for d in (2, 1, 3)]
         for c in batch:
             c.start()
@@ -442,8 +442,8 @@
     keep.start()
 
     def far_body(i, carry):
-        for w in range(4):
-            t = i * 4 + w
+        for w in range(8):
+            t = i * 8 + w
             p = zp[t]
             s = swap(p)
             zero = jnp.zeros_like(p)
@@ -459,7 +459,7 @@
                 far_ref[2 * pair + 1] = r[8:]
         return carry
 
-    lax.fori_loop(0, leaves // 16, far_body, 0)
+    lax.fori_loop(0, leaves // 32, far_body, 0)
     keep.wait()
     for c in nears:
         c.wait_recv()

time: 32.2 us -> 30.9 us (0.960)
  Pallas kernels: 32 us -> 30.8 us
    pallas_call x1, Pallas kernels: 27.5 us -> 26.3 us  [local(): pl.pallas_call(functools.partial(main_kernel, n_leaf, n_vec), out_shape=(...]
where the time goes in v5:
time: 30.9 us; the launch traced here: 30.8 us
  Pallas kernels  30.8 us (100%)
    pallas_call x1, Pallas kernels, local(): pl.pallas_call(functools.partial(main_kernel, n_leaf, n_vec), out_shape=(...  26.3 us
    pallas_call x1, Pallas kernels, local(): pl.pallas_call(restore_kernel, out_shape=jax.ShapeDtypeStruct(panels.shap...  2.47 us
    pallas_call x1, Pallas kernels, local(): pl.pallas_call(order_kernel, out_shape=jax.ShapeDtypeStruct((leaves, rows...  1.97 us

profile of v5, /device:TPU:0, one launch (start us, length us, event | category | flops | bytes accessed | tf_op | source)
XLA Modules:
  0.0 30.8 jit_solution(14717456196884482764)
XLA Ops:
  0.0 2.0 %order.1.own_ref = f32[64,8,128]{2,1,0:T(8,128)} custom-call(f32[8,8192]{1,0:T(8,128)} %panels_ref.1, s32[64,128]{1,0:T(8,128)} %order_ref.3), custom_call_target="tpu_custom_call" | custom-call | tf_op jit(solution)/shard_map/order/pallas_call | solution.py:488
  2.0 26.3 %tree.1 = (f32[64,8,128]{2,1,0:T(8,128)}, f32[4,16,8,128]{3,2,1,0:T(8,128)}, f32[64,8,128]{2,1,0:T(8,128)}) custom-call(f32[64,8,128]{2,1,0:T(8,128)} %order.1.own_ref, s32[64,128]{1,0:T(8,128)} %order_ref.3, s32[4,64]{1,0:T(4,128)} %bitcast.5, s32[1,63]{1,0:T(1,128)} %flags_hbm.1, s32[6]{0:T(128)} %cross_flags_hbm.1, f32[6,64,64]{2,1,0:T(8,128)} %cross_c_hbm.1, ...), custom_call_target="tpu_custom_call" | custom-call | tf_op jit(solution)/shard_map/tree/pallas_call | solution.py:499
  28.3 2.5 %restore.1 = f32[8,8192]{1,0:T(8,128)} custom-call(f32[64,8,128]{2,1,0:T(8,128)} %get-tuple-element.8.far_ref, f32[4,16,8,128]{3,2,1,0:T(8,128)} %get-tuple-element.9.near_ref, f32[64,8,128]{2,1,0:T(8,128)} %get-tuple-element.10.inverse_ref), custom_call_target="tpu_custom_call" | custom-call | tf_op jit(solution)/shard_map/restore/pallas_call | solution.py:550
